TPU v7x, 128 devices: a whole 4x4x4 slice. The times are simulated.
128 devices in a mesh: slab: 16 (over x, z), tile: 8 (over y, core).
Axes of the slice: x: 4, y: 4, z: 4, core: 2. Of those that a mesh axis runs over, the one named last changes fastest.
Arguments:
- encoded: bfloat16 [16, 16, 4096, 128], P('slab', None, 'tile'), may hold values from -6 to 6
- spacing: float32 [16, 16, 4096], P('slab', None, 'tile'), may hold values from 0.002 to 0.05
- counts: int32 [16, 4096], P('slab', 'tile'), may hold values from 1 to 16
- seg_first: int32 [4096], P('tile'), may hold values from 0 to 3
- seg_last: int32 [4096], P('tile'), may hold values from 13 to 16
- direction: int32 [4096], P('tile'), may hold values from 0 to 1
- field_in: bfloat16 [16, 128, 256], P('slab'), may hold values from -0.5 to 0.5
- field_mid: bfloat16 [16, 256, 256], P('slab'), may hold values from -0.375 to 0.375
- field_out: bfloat16 [16, 256, 64], P('slab'), may hold values from -0.375 to 0.375
- color_head: float32 [64, 3], replicated, may hold values from -0.75 to 0.75
- target: float32 [4096, 3], P('tile'), may hold values from 0 to 1
Outputs:
- front_trans: float32 [16, 4096], P('slab', 'tile')
- grad_in: float32 [16, 128, 256], P('slab')
- grad_mid: float32 [16, 256, 256], P('slab')
- grad_out: float32 [16, 256, 64], P('slab')
All inputs are finite; a program needn't handle non-finite values.
Results may differ from a plain program's by a relative error of at most 0.014.
The roundings to bfloat16 on the way count: a program that leaves them out, or rounds other values in their place, can miss the bound.
Values sent between devices are 32-bit elements; how exact they have to be, the bound alone decides.
A program may use at most 64 MiB of HBM per device.

v0:
```python
import jax
import jax.numpy as jnp
from jax import lax
from jax.sharding import PartitionSpec as P


def field(field_in, field_mid, field_out, inputs):
    hidden_one = jax.nn.relu(jnp.dot(inputs, field_in, preferred_element_type=jnp.float32)).astype(
        jnp.bfloat16
    )
    hidden_two = jax.nn.relu(
        jnp.dot(hidden_one, field_mid, preferred_element_type=jnp.float32)
    ).astype(jnp.bfloat16)
    outputs = jnp.dot(hidden_two, field_out, preferred_element_type=jnp.float32)
    return (hidden_one, hidden_two, outputs)


def composite(outputs, spacing, live_mask, direction):
    optical = jax.nn.softplus(outputs[:, :, 0]) * spacing * live_mask
    running = jnp.cumsum(optical, axis=0)
    column_sum = running[-1]
    before = jnp.where(direction[None, :] > 0, column_sum[None, :] - running, running - optical)
    weights = jnp.exp(-before) * (1.0 - jnp.exp(-optical))
    colors = jnp.sum(weights[:, :, None] * outputs, axis=0)
    return (jnp.exp(-column_sum), colors)


def make_combine(front_first):

    def combine(earlier, later):
        trans_early, color_early = earlier
        trans_late, color_late = later
        joined = jnp.where(
            front_first[:, None],
            color_early + trans_early[:, None] * color_late,
            color_late + trans_late[:, None] * color_early,
        )
        return (trans_early * trans_late, joined)

    return combine


def field_grads(field_mid, field_out, inputs, hidden_one, hidden_two, grad_outputs):
    grad_low = grad_outputs.astype(jnp.bfloat16)
    grad_three = jnp.dot(hidden_two.T, grad_low, preferred_element_type=jnp.float32)
    back_two = (
        jnp.dot(grad_low, field_out.T, preferred_element_type=jnp.float32) * (hidden_two > 0)
    ).astype(jnp.bfloat16)
    grad_two = jnp.dot(hidden_one.T, back_two, preferred_element_type=jnp.float32)
    back_one = (
        jnp.dot(back_two, field_mid.T, preferred_element_type=jnp.float32) * (hidden_one > 0)
    ).astype(jnp.bfloat16)
    grad_one = jnp.dot(inputs.T, back_one, preferred_element_type=jnp.float32)
    return (grad_one, grad_two, grad_three)


def pixel_grad(color_total, color_head, target, ray_count):
    logits = jnp.dot(color_total, color_head, precision=lax.Precision.HIGHEST)
    shade = jax.nn.sigmoid(logits)
    error = (shade - target) / ray_count
    return jnp.dot(error * shade * (1.0 - shade), color_head.T, precision=lax.Precision.HIGHEST)


def body(
    encoded,
    spacing,
    counts,
    seg_first,
    seg_last,
    direction,
    field_in,
    field_mid,
    field_out,
    color_head,
    target,
):
    samples = encoded.shape[1]
    ray_count = encoded.shape[2]
    width_in = encoded.shape[3]
    width_out = field_out.shape[2]
    my_slab = lax.axis_index("slab")
    reverse_rays = direction > 0
    active = (seg_first <= my_slab) & (my_slab < seg_last)
    sample_ids = jnp.arange(samples, dtype=jnp.int32)
    live_mask = ((sample_ids[:, None] < counts[0][None, :]) & active[None, :]).astype(jnp.float32)
    inputs = encoded[0].reshape(-1, width_in)
    hidden_one, hidden_two, outputs = field(field_in[0], field_mid[0], field_out[0], inputs)
    outputs_three = outputs.reshape(samples, ray_count, width_out)
    own_trans, own_color = composite(outputs_three, spacing[0], live_mask, direction)
    combine_low = make_combine(jnp.logical_not(reverse_rays))
    identity = (jnp.ones((ray_count,), jnp.float32), jnp.zeros((ray_count, width_out), jnp.float32))
    every_trans, every_color = (
        lax.all_gather(own_trans[None], "slab", axis=0, tiled=True),
        lax.all_gather(own_color[None], "slab", axis=0, tiled=True),
    )
    slab_ids = jnp.arange(every_trans.shape[0], dtype=jnp.int32)

    def step_low(running_pair, item):
        item_trans, item_color, item_slab = item
        keep = item_slab < my_slab
        masked = (jnp.where(keep, item_trans, 1.0), jnp.where(keep, item_color, 0.0))
        return (combine_low(running_pair, masked), None)

    def step_high(running_pair, item):
        item_trans, item_color, item_slab = item
        keep = item_slab > my_slab
        masked = (jnp.where(keep, item_trans, 1.0), jnp.where(keep, item_color, 0.0))
        return (make_combine(reverse_rays)(running_pair, masked), None)

    low_pair, _ = lax.scan(step_low, identity, (every_trans, every_color, slab_ids))
    high_pair, _ = lax.scan(step_high, identity, (every_trans, every_color, slab_ids), reverse=True)
    front_trans = jnp.where(reverse_rays, high_pair[0], low_pair[0])
    front_color = jnp.where(reverse_rays[:, None], high_pair[1], low_pair[1])
    back_color = jnp.where(reverse_rays[:, None], low_pair[1], high_pair[1])
    color_total = (
        front_color
        + front_trans[:, None] * own_color
        + (front_trans * own_trans)[:, None] * back_color
    )
    grad_color = pixel_grad(color_total, color_head, target, ray_count)
    grad_seg_color = front_trans[:, None] * grad_color
    grad_seg_trans = front_trans * jnp.sum(grad_color * back_color, axis=1)
    space_here = spacing[0]
    _, pull_back = jax.vjp(
        lambda values: composite(values, space_here, live_mask, direction), outputs_three
    )
    grad_outputs = pull_back((grad_seg_trans, grad_seg_color))[0].reshape(-1, width_out)
    grad_one, grad_two, grad_three = field_grads(
        field_mid[0], field_out[0], inputs, hidden_one, hidden_two, grad_outputs
    )
    grad_one, grad_two, grad_three = lax.psum((grad_one, grad_two, grad_three), "tile")
    return (front_trans[None], grad_one[None], grad_two[None], grad_three[None])


def solution(mesh):
    return jax.shard_map(
        body,
        mesh=mesh,
        in_specs=(
            P("slab", None, "tile", None),
            P("slab", None, "tile"),
            P("slab", "tile"),
            P("tile"),
            P("tile"),
            P("tile"),
            P("slab", None, None),
            P("slab", None, None),
            P("slab", None, None),
            P(),
            P("tile", None),
        ),
        out_specs=(
            P("slab", "tile"),
            P("slab", None, None),
            P("slab", None, None),
            P("slab", None, None),
        ),
        check_vma=False,
    )
```

profile of v0, /device:TPU:1, one launch (start us, length us, event | category | flops | bytes accessed | tf_op | source)
XLA Modules:
  0.0 246.2 jit_solution(4102915026123431221)
XLA Ops:
  7.2 1.5 copy-done
  8.8 2.1 fusion.4
  12.9 1.9 copy-done.3
  14.8 1.4 fusion.40
  16.2 1.3 copy-done.5
  19.0 2.5 %multiply_reduce_fusion.1 = f32[512,64]{0,1:T(8,128)} fusion(f32[16,512,64]{1,2,0:T(8,128)} %copy-done.5, f32[16,512]{1,0:T(8,128)S(1)} %bitcast.117), kind=kLoop, calls=%fused_computation.22 | loop fusion | flops 1015808 | bytes 2260992 | tf_op jit(solution)/shard_map/reduce_sum | solution.py:24
  21.6 20.7 %all-gather.1 = f32[16,1,512]{2,1,0:T(1,128)S(1)} all-gather(f32[1,1,512]{2,1,0:T(1,128)S(1)} %get-tuple-element.373), channel_id=1, replica_groups=mesh['slab'=16,'tile'=8] {'slab'}, dimensions={0}, use_global_device_ids=true | all-gather | bytes 34816 | tf_op jit(solution)/shard_map/all_gather | solution.py:93
  42.3 26.8 %all-gather.4.cloned.1.call-done = f32[8192,64]{0,1:T(8,128)} async-done(((f32[512,64]{0,1:T(8,128)}), f32[8192,64]{0,1:T(8,128)}) %all-gather.4.cloned.1.call-update) | async-done | bytes 2097168 | tf_op jit(solution)/shard_map/all_gather | solution.py:94
  69.1 3.8 %copy.41 = f32[8192,64]{1,0:T(8,128)} copy(f32[8192,64]{0,1:T(8,128)} %all-gather.4.cloned.1.call-done) | data formatting | bytes 4194304
  72.9 42.9 %while.31 = (s32[]{:T(128)}, f32[512]{0:T(512)S(1)}, f32[512,64]{1,0:T(8,128)S(1)}, s32[16]{0:T(128)S(1)}, s32[]{:T(128)}, /*index=5*/f32[16,512]{1,0:T(8,128)S(...) while((s32[]{:T(128)}, f32[512]{0:T(512)S(1)}, ...), condition=%wide.region_5.6_spmd.clone, body=%wide.region_4.5_spmd.clone.sunk | while | flops 230916 | bytes 410255 | solution.py:110
  74.3 1.3 fusion.80
  77.0 1.3 fusion.80
  79.7 1.3 fusion.80
  82.4 1.3 fusion.80
  93.1 1.3 fusion.80
  95.8 1.3 fusion.80
  98.5 1.3 fusion.80
  101.1 1.3 fusion.80
  103.8 1.3 fusion.80
  106.5 1.3 fusion.80
  116.0 41.0 %while.30 = (s32[]{:T(128)}, f32[512]{0:T(512)S(1)}, f32[512,64]{1,0:T(8,128)S(1)}, s32[16]{0:T(128)S(1)}, s32[]{:T(128)}, /*index=5*/f32[16,512]{1,0:T(8,128)S(...) while((s32[]{:T(128)}, f32[512]{0:T(512)S(1)}, ...), condition=%wide.region_3.4_spmd.clone, body=%wide.region_2.3_spmd.clone.sunk | while | flops 230917 | bytes 410275 | solution.py:111
  157.8 2.2 multiply_reduce_fusion
  160.1 1.5 fusion.15
  161.9 1.4 convolution_bitcast_fusion.1
  163.4 1.3 fusion.6
  164.7 2.0 copy-done.6
  166.6 2.0 convolution_bitcast_fusion
  168.6 6.7 %fusion.9 = f32[1,128,256]{1,2,0:T(8,128)} fusion(bf16[8192,128]{1,0:T(8,128)(2,1)S(1)} %bitcast.108, bf16[8192,256]{1,0:T(8,128)(2,1)} %copy-done.6, bf16[8192,256]{1,0:T(8,128)(2,1)} %copy-done.1, bf16[1,256,256]{2,1,0:T(8,128)(2,1)S(1)} %copy-done.9), kind=kOutput, calls=%fused_computation.25 | convolution fusion | flops 1616904192 | bytes 10747904 | tf_op jit(solution)/shard_map/dot_general | solution.py:53
  175.4 59.2 %all-reduce.5.cloned.1.call-done = (f32[1,128,256]{1,2,0:T(8,128)}, f32[1,256,256]{2,1,0:T(8,128)}, f32[1,256,64]{1,2,0:T(8,128)}) async-done(((f32[1,128,256]{1,2,0:T(8,128)}, f32[1,256,256]{2,1,0:T(8,128)}, f32[1,256,64]{1,2,0:T(8,128)}), (f32[1,128,256]{1,2,0:T(8,128)}, f32[1,256,256]{2,1,0:T(8,128)}, f32[1,256,64]{1,2,0:T(8,128)})) %all-reduce.5.cloned.1.call-update) | async-done | bytes 458768 | tf_op jit(solution)/shard_map/psum | solution.py:131
  234.6 1.7 copy.40
  236.2 1.7 copy.74
  237.9 1.5 copy.75
  (182 shorter events, 53.3 us)
Async XLA Ops:
  7.2 1.6 copy-start
  7.2 61.9 %all-gather.4.cloned.1.call-start = ((), (), s32[]{:S(2)}) async-start(), calls=%async_computation | async-start | bytes 2228224 | tf_op jit(solution)/shard_map/all_gather | solution.py:94
  8.8 2.1 copy-start.9
  10.9 1.9 copy-start.1
  10.9 3.9 %copy-start.10 = (bf16[1,256,64]{1,2,0:T(8,128)(2,1)S(1)}, bf16[1,256,64]{1,2,0:T(8,128)(2,1)}, u32[]{:S(2)}) copy-start(bf16[1,256,64]{1,2,0:T(8,128)(2,1)} %param.23) | copy-start | bytes 98308
  12.8 2.0 copy-start.3
  12.8 4.7 %copy-start.16 = (s32[512]{0:T(512)S(1)}, s32[512]{0:T(512)}, u32[]{:S(2)}) copy-start(s32[512]{0:T(512)} %param.19) | copy-start | bytes 6148
  12.8 4.7 %copy-start.17 = (s32[512]{0:T(512)S(1)}, s32[512]{0:T(512)}, u32[]{:S(2)}) copy-start(s32[512]{0:T(512)} %param.18) | copy-start | bytes 6148
  12.8 4.7 %copy-start.8 = (f32[1,16,512]{2,1,0:T(8,128)S(1)}, f32[1,16,512]{2,1,0:T(8,128)}, u32[]{:S(2)}) copy-start(f32[1,16,512]{2,1,0:T(8,128)} %param.16) | copy-start | bytes 98308
  12.8 4.7 %copy-start.12 = (s32[1,512]{1,0:T(1,128)S(1)}, s32[1,512]{1,0:T(1,128)}, u32[]{:S(2)}) copy-start(s32[1,512]{1,0:T(1,128)} %param.17) | copy-start | bytes 6148
  12.9 4.8 %copy-start.15 = (s32[512]{0:T(512)S(1)}, s32[512]{0:T(512)}, u32[]{:S(2)}) copy-start(s32[512]{0:T(512)} %param.20) | copy-start | bytes 6148
  16.2 1.3 copy-start.5
  21.5 213.1 %all-reduce.5.cloned.1.call-start = ((), (), s32[]{:S(2)}) async-start(), calls=%async_computation.1 | async-start | bytes 917504 | tf_op jit(solution)/shard_map/psum | solution.py:131
  72.9 84.3 %copy-start.7 = (f32[512,64]{0,1:T(8,128)S(1)}, f32[512,64]{0,1:T(8,128)}, u32[]{:S(2)}) copy-start(f32[512,64]{0,1:T(8,128)} %multiply_reduce_fusion.1) | copy-start | bytes 393220
  72.9 84.3 %copy-start.13 = (f32[64,3]{0,1:T(4,128)S(1)}, f32[64,3]{0,1:T(4,128)}, u32[]{:S(2)}) copy-start(f32[64,3]{0,1:T(4,128)} %param.24) | copy-start | bytes 2308
  72.9 84.5 %copy-start.14 = (f32[512,3]{0,1:T(4,128)S(1)}, f32[512,3]{0,1:T(4,128)}, u32[]{:S(2)}) copy-start(f32[512,3]{0,1:T(4,128)} %param.25) | copy-start | bytes 18436
  157.1 4.8 %copy-start.4 = (bf16[8192,256]{1,0:T(8,128)(2,1)S(1)}, bf16[8192,256]{1,0:T(8,128)(2,1)}, u32[]{:S(2)}) copy-start(bf16[8192,256]{1,0:T(8,128)(2,1)} %copy-done.3) | copy-start | bytes 12582916
  157.2 6.2 %copy-start.11 = (f32[512]{0:T(512)}, f32[512]{0:T(512)S(1)}, u32[]{:S(2)}) copy-start(f32[512]{0:T(512)S(1)} %get-tuple-element.368) | copy-start | bytes 6148
  163.4 3.3 %copy-start.2 = (bf16[8192,256]{1,0:T(8,128)(2,1)S(1)}, bf16[8192,256]{1,0:T(8,128)(2,1)}, u32[]{:S(2)}) copy-start(bf16[8192,256]{1,0:T(8,128)(2,1)} %copy-done.1) | copy-start | bytes 12582916
  164.7 2.0 copy-start.6
Sparse Core Ops, SparseCore 0:
  21.6 47.4 all-gather.3
  175.5 59.0 all-reduce.4
where the time goes:
time: 249 us; the launch traced here: 246 us
  waiting for transfers between devices  86 us (35%)
  other arithmetic  49 us (20%)
  local copies, waits for them, and re-layouts  36.5 us (15%)
  loops' own time  22.8 us (9%)
  blocking collectives  20.7 us (8%)
  matrix products  16.7 us (7%)
  between operations  14.4 us (6%)
    psum x1, waiting for transfers between devices, body(): lax.psum((grad_one, grad_two, grad_three), 'tile')  59.2 us
    select_n x32, other arithmetic, combine(): jnp.where(front_first[:, None], color_early + trans_early[:, None] * colo...  40.3 us
    all_gather x1, waiting for transfers between devices, body(): lax.all_gather(own_color[None], 'slab', axis=0, tiled=True)  26.8 us
    all_gather x1, blocking collectives, body(): lax.all_gather(own_trans[None], 'slab', axis=0, tiled=True)  20.7 us
    dynamic_slice x32, local copies, waits for them, and re-layouts, body(): lax.scan(step_low, identity, (every_trans, every_color, slab_ids))  20 us
    unnamed x42, local copies, waits for them, and re-layouts  16.1 us
    another operation x1, loops' own time, body(): lax.scan(step_low, identity, (every_trans, every_color, slab_ids))  11.7 us
    another operation x1, loops' own time, body(): lax.scan(step_high, identity, (every_trans, every_color, slab_ids), rever...  11.1 us
  transfers between devices with their start and end apart: 2, of which 2 were waited for; matrix products, arithmetic and copies ran while one was open for 0% of the time, Pallas kernels for 0%

commit v1 on v0

v1 whole, which is shorter than its diff:
```python
import functools

import jax
import jax.numpy as jnp
from jax import lax
from jax.experimental import pallas as pl
from jax.experimental.pallas import tpu as pltpu
from jax.sharding import PartitionSpec as P

MESH = pl.DeviceIdType.MESH
NN = ((1,), (0,))
NT = ((1,), (1,))
LANES = 128


def mm(a, b, dims):
    return lax.dot_general(a, b, (dims, ((), ())), preferred_element_type=jnp.float32)


def running_sum(values):
    rows = values.shape[0]
    row_ids = lax.broadcasted_iota(jnp.int32, values.shape, 0)
    shift = 1
    while shift < rows:
        moved = pltpu.roll(values, shift, axis=0)
        values = values + jnp.where(row_ids >= shift, moved, 0.0)
        shift *= 2
    return values


def kernel(
    chunks,
    n_slab,
    n_tile,
    x_hbm,
    space_hbm,
    counts_hbm,
    first_hbm,
    last_hbm,
    dir_hbm,
    w1_hbm,
    w2_hbm,
    w3t_hbm,
    head_hbm,
    target_hbm,
    front_out,
    g1_out,
    g2_out,
    g3_out,
    x_s,
    space_s,
    ints_s,
    w1_s,
    w2_s,
    w3t_s,
    head_s,
    target_s,
    w1t_s,
    w2t_s,
    w3_s,
    head8_s,
    headt_s,
    w3p_s,
    h1_s,
    h2_s,
    b2_s,
    gl_s,
    proj_s,
    saved_s,
    row_s,
    send_s,
    gather_s,
    g1_s,
    g1t_s,
    g2_s,
    g3_s,
    half1_s,
    half2_s,
    half3_s,
    pair1_s,
    pair2_s,
    pair3_s,
    quad1_s,
    quad2_s,
    quad3_s,
    in_sem,
    ex_send,
    ex_recv,
    pair_send,
    pair_recv,
    quad_send,
    quad_recv,
    ag_send,
    ag_recv,
):
    samples, rays_dev = space_s.shape
    rays = rays_dev // chunks
    cols = samples * rays
    groups = rays // LANES
    me = lax.axis_index("slab")
    tile = lax.axis_index("tile")
    core, ypos = tile % 2, tile // 2
    n_y = n_tile // 2

    barrier = pltpu.get_barrier_semaphore()
    for step in range(1, n_slab):
        pl.semaphore_signal(
            barrier, inc=1, device_id={"slab": (me + step) % n_slab}, device_id_type=MESH
        )
    mates = [(ypos * 2 + 1 - core)] + [((ypos + d) % n_y) * 2 + core for d in range(1, n_y)]
    for mate in mates:
        pl.semaphore_signal(barrier, inc=1, device_id={"tile": mate}, device_id_type=MESH)

    small = [
        (w1_hbm.at[0], w1_s),
        (w2_hbm.at[0], w2_s),
        (w3t_hbm.at[0], w3t_s),
        (head_hbm, head_s),
        (space_hbm.at[0], space_s),
        (counts_hbm, ints_s.at[0]),
        (first_hbm, ints_s.at[1]),
        (last_hbm, ints_s.at[2]),
        (dir_hbm, ints_s.at[3]),
        (target_hbm, target_s),
    ]
    loads = [
        pltpu.make_async_copy(src, dst, in_sem.at[chunks + i]) for i, (src, dst) in enumerate(small)
    ]
    x_loads = [
        pltpu.make_async_copy(
            x_hbm.at[0, :, pl.ds(c * rays, rays), :], x_s.at[c], in_sem.at[c]
        )
        for c in range(chunks)
    ]
    loads[0].start()
    x_loads[0].start()
    for load in loads[1:]:
        load.start()
    for load in x_loads[1:]:
        load.start()

    loads[0].wait()
    w1t_s[...] = w1_s[...].T
    loads[1].wait()
    w2t_s[...] = w2_s[...].T
    loads[2].wait()
    w3_s[...] = w3t_s[...].T
    loads[3].wait()
    head8_s[...] = jnp.zeros_like(head8_s)
    lane = lax.broadcasted_iota(jnp.int32, (1, LANES), 1)
    head8_s[0:1, :] = (lane == 0).astype(jnp.float32)
    head8_s[1:4, 0 : head_s.shape[1]] = head_s[...]
    headt_s[...] = head8_s[...].T
    width = w3t_s.shape[0]
    folded = lax.dot_general(
        head8_s[:, 0:width],
        w3t_s[...].astype(jnp.float32),
        (NN, ((), ())),
        precision=lax.Precision.HIGHEST,
        preferred_element_type=jnp.float32,
    )
    hi = folded.astype(jnp.bfloat16)
    rest = folded - hi.astype(jnp.float32)
    mid = rest.astype(jnp.bfloat16)
    low = (rest - mid.astype(jnp.float32)).astype(jnp.bfloat16)
    w3p_s[...] = jnp.concatenate(
        [hi.astype(jnp.float32), mid.astype(jnp.float32), low.astype(jnp.float32), jnp.zeros_like(folded)],
        axis=0,
    ).astype(jnp.bfloat16)
    for load in loads[4:]:
        load.wait()

    row_ids = lax.broadcasted_iota(jnp.int32, (samples, rays), 0)
    tile_rows = lax.broadcasted_iota(jnp.int32, (8, LANES), 0)
    is_trans = (tile_rows % 4) == 0
    identity = is_trans.astype(jnp.float32)

    def spread(v):
        return jnp.where(tile_rows < 4, v[0:1, :], v[4:5, :])

    def ray_slice(c):
        return pl.ds(c * rays, rays)

    def exchange(c, step):
        peer = (me + step) % n_slab
        return pltpu.make_async_remote_copy(
            src_ref=send_s.at[c],
            dst_ref=gather_s.at[c, me],
            send_sem=ex_send.at[c, step],
            recv_sem=ex_recv.at[c, me],
            device_id={"slab": peer},
            device_id_type=MESH,
        )

    def forward(c):
        x_loads[c].wait()
        x = x_s[c].reshape(cols, x_s.shape[3])
        base = c * cols
        h1 = jnp.maximum(mm(w1t_s[...], x, NT).astype(jnp.bfloat16), 0)
        h1_s[:, pl.ds(base, cols)] = h1
        h2 = jnp.maximum(mm(w2t_s[...], h1, NN).astype(jnp.bfloat16), 0)
        h2_s[:, pl.ds(base, cols)] = h2
        p = mm(w3p_s[...], h2, NN)
        p = p[0:8, :] + (p[8:16, :] + p[16:24, :])
        for j in range(samples):
            for g in range(groups):
                at = j * rays + g * LANES
                proj_s[g, 8 * j : 8 * j + 8, :] = p[:, at : at + LANES]
        o0, *ps = (
            jnp.concatenate(
                [proj_s[g, pl.ds(k, samples, stride=8), :] for g in range(groups)], 1
            )
            for k in range(4)
        )
        rs = ray_slice(c)
        counts = ints_s[0, :, rs]
        first = ints_s[1, :, rs]
        last = ints_s[2, :, rs]
        reverse = ints_s[3, :, rs] > 0
        active = (first <= me) & (me < last)
        live = ((row_ids < counts) & active).astype(jnp.float32)
        span = space_s[:, rs] * live
        soft = jnp.maximum(o0, 0.0) + jnp.log1p(jnp.exp(-jnp.abs(o0)))
        optical = soft * span
        running = running_sum(optical)
        column = running[samples - 1 : samples, :]
        before = jnp.where(reverse, column - running, running - optical)
        gone = jnp.exp(-before)
        stay = jnp.exp(-optical)
        weights = gone * (1.0 - stay)
        trans = jnp.exp(-column)
        saved_s[c, 0] = weights
        saved_s[c, 1] = gone * stay
        saved_s[c, 2] = span * (1.0 / (1.0 + jnp.exp(-o0)))
        for k in range(3):
            saved_s[c, 3 + k] = ps[k]
        row_s[c] = trans
        rows = [trans] + [jnp.sum(weights * ps[k], axis=0, keepdims=True) for k in range(3)]
        for g in range(groups):
            for k in range(4):
                send_s[c, 4 * g + k : 4 * g + k + 1, :] = rows[k][:, g * LANES : (g + 1) * LANES]
        gather_s[c, me] = send_s[c]
        if c == 0:
            pl.semaphore_wait(barrier, n_slab - 1 + len(mates))
        for step in range(1, n_slab):
            exchange(c, step).start()

    def compose(c):
        for step in range(1, n_slab):
            source = (me + n_slab - step) % n_slab
            pltpu.make_async_remote_copy(
                src_ref=send_s.at[c],
                dst_ref=gather_s.at[c, source],
                send_sem=ex_send.at[c, step],
                recv_sem=ex_recv.at[c, source],
                device_id={"slab": source},
                device_id_type=MESH,
            ).wait_recv()
        rs = ray_slice(c)
        reverse = ints_s[3, :, rs] > 0
        rev = jnp.where(
            tile_rows < 4,
            jnp.broadcast_to(ints_s[3, :, pl.ds(c * rays, LANES)], (8, LANES)),
            jnp.broadcast_to(ints_s[3, :, pl.ds(c * rays + (groups - 1) * LANES, LANES)], (8, LANES)),
        ) > 0

        def step_of(run, item, item_first):
            run_t, item_t = spread(run), spread(item)
            run_first = jnp.where(is_trans, 0.0, run) + run_t * item
            late_first = jnp.where(is_trans, 0.0, item) + item_t * run
            return jnp.where(item_first, late_first, run_first)

        low = identity
        for s in range(n_slab):
            low = step_of(low, jnp.where(s < me, gather_s[c, s], identity), rev)
        high = identity
        for s in reversed(range(n_slab)):
            high = step_of(high, jnp.where(s > me, gather_s[c, s], identity), jnp.logical_not(rev))
        own = gather_s[c, me]
        front = jnp.where(rev, high, low)
        back = jnp.where(rev, low, high)
        front_t, own_t = spread(front), spread(own)
        logits = front + front_t * own + (front_t * own_t) * back
        shade = 1.0 / (1.0 + jnp.exp(-logits))
        target = jnp.zeros((8, LANES), jnp.float32)
        for g in range(groups):
            for k in range(3):
                target = jnp.where(
                    tile_rows == 4 * g + 1 + k,
                    target_s[k : k + 1, pl.ds(c * rays + g * LANES, LANES)],
                    target,
                )
        grad3 = jnp.where(is_trans, 0.0, (shade - target) * (1.0 / rays_dev) * shade * (1.0 - shade))
        dots = grad3 * back
        fronts, grads, seg_t = [], [[], [], []], []
        for g in range(groups):
            r = 4 * g
            fronts.append(front[r : r + 1, :])
            for k in range(3):
                grads[k].append(grad3[r + 1 + k : r + 2 + k, :])
            seg_t.append(dots[r + 1 : r + 2, :] + dots[r + 2 : r + 3, :] + dots[r + 3 : r + 4, :])
        join = lambda parts: jnp.concatenate(parts, 1)
        front_row = join(fronts)
        front_out[:, rs] = front_row
        grad_rows = [front_row * join(grads[k]) for k in range(3)]
        return reverse, grad_rows, front_row * join(seg_t)

    def backward(c):
        reverse, grad_rows, grad_trans = compose(c)
        weights, spent = saved_s[c, 0], saved_s[c, 1]
        grad_w = (
            grad_rows[0] * saved_s[c, 3] + grad_rows[1] * saved_s[c, 4] + grad_rows[2] * saved_s[c, 5]
        )
        pulled = weights * grad_w
        running = running_sum(pulled)
        total = running[samples - 1 : samples, :]
        later = jnp.where(reverse, running - pulled, total - running)
        grad_optical = spent * grad_w - row_s[c] * grad_trans - later
        grad_density = grad_optical * saved_s[c, 2]
        grad_color = (
            headt_s[0:width, 1:2] * grad_rows[0]
            + headt_s[0:width, 2:3] * grad_rows[1]
            + headt_s[0:width, 3:4] * grad_rows[2]
        )
        first_row = lax.broadcasted_iota(jnp.int32, (width, 1), 0) == 0
        base = c * cols
        for j in range(samples):
            at = pl.ds(base + j * rays, rays)
            gl_s[:, at] = (
                grad_color * weights[j : j + 1, :]
                + jnp.where(first_row, grad_density[j : j + 1, :], 0.0)
            ).astype(jnp.bfloat16)
        b2 = mm(w3_s[...], gl_s[:, pl.ds(base, cols)], NN).astype(jnp.bfloat16)
        b2 = jnp.where(h2_s[:, pl.ds(base, cols)] > 0, b2, 0)
        b2_s[:, pl.ds(base, cols)] = b2
        part = mm(h1_s[:, pl.ds(base, cols)], b2, NT)
        g2_s[...] = part if c == 0 else g2_s[...] + part

    def backward_one(c):
        base = c * cols
        b1 = mm(w2_s[...], b2_s[:, pl.ds(base, cols)], NN).astype(jnp.bfloat16)
        b1 = jnp.where(h1_s[:, pl.ds(base, cols)] > 0, b1, 0)
        part = mm(b1, x_s[c].reshape(cols, x_s.shape[3]), NN)
        g1t_s[...] = part if c == 0 else g1t_s[...] + part

    grads = (
        (g1_s, half1_s, pair1_s, quad1_s, g1_out),
        (g2_s, half2_s, pair2_s, quad2_s, g2_out),
        (g3_s, half3_s, pair3_s, quad3_s, g3_out),
    )

    def piece_rows(i, k, y):
        rows = grads[i][0].shape[0]
        return pl.ds(pl.multiple_of(k * (rows // 2) + y * (rows // n_tile), 8), rows // n_tile)

    def pair_copy(i):
        whole, half, pair = grads[i][:3]
        rows = half.shape[0]
        return pltpu.make_async_remote_copy(
            src_ref=whole.at[pl.ds(pl.multiple_of((1 - core) * rows, 8), rows), :],
            dst_ref=pair,
            send_sem=pair_send.at[i],
            recv_sem=pair_recv.at[i],
            device_id={"tile": ypos * 2 + 1 - core},
            device_id_type=MESH,
        )

    def pair_sum(i):
        whole, half, pair = grads[i][:3]
        rows = half.shape[0]
        pair_copy(i).wait_recv()
        half[...] = whole[pl.ds(pl.multiple_of(core * rows, 8), rows), :] + pair[...]

    def quad_copy(i, d):
        half, quad = grads[i][1], grads[i][3]
        rows = quad.shape[1]
        to = (ypos + d) % n_y
        return pltpu.make_async_remote_copy(
            src_ref=half.at[pl.ds(pl.multiple_of(to * rows, 8), rows), :],
            dst_ref=quad.at[d],
            send_sem=quad_send.at[i, d],
            recv_sem=quad_recv.at[i, d],
            device_id={"tile": to * 2 + core},
            device_id_type=MESH,
        )

    def quad_sum(i):
        half, quad, out = grads[i][1], grads[i][3], grads[i][4]
        rows = quad.shape[1]
        total = half[pl.ds(pl.multiple_of(ypos * rows, 8), rows), :]
        for d in range(1, n_y):
            quad_copy(i, d).wait_recv()
            total = total + quad[d]
        out[piece_rows(i, core, ypos), :] = total

    def gather_copy(i, y, to_tile, sem):
        out = grads[i][4]
        at = piece_rows(i, core, y)
        return pltpu.make_async_remote_copy(
            src_ref=out.at[at, :],
            dst_ref=out.at[at, :],
            send_sem=ag_send.at[i, sem],
            recv_sem=ag_recv.at[i, y * 2 + core],
            device_id={"tile": to_tile},
            device_id_type=MESH,
        )

    def gather_start(i):
        gather_copy(i, ypos, ypos * 2 + 1 - core, 0).start()
        for d in range(1, n_y):
            gather_copy(i, ypos, ((ypos + d) % n_y) * 2 + core, d).start()

    def gather_wait(i, k, y):
        out = grads[i][4]
        at = piece_rows(i, k, y)
        pltpu.make_async_remote_copy(
            src_ref=out.at[at, :],
            dst_ref=out.at[at, :],
            send_sem=ag_send.at[i, 0],
            recv_sem=ag_recv.at[i, y * 2 + k],
            device_id={"tile": ypos * 2 + 1 - core},
            device_id_type=MESH,
        ).wait_recv()

    def gather_forward(i):
        for d in range(1, n_y):
            y = (ypos + n_y - d) % n_y
            gather_wait(i, core, y)
            gather_copy(i, y, ypos * 2 + 1 - core, n_y - 1 + d).start()

    def gather_finish(i):
        for y in range(n_y):
            gather_wait(i, 1 - core, y)
        gather_copy(i, ypos, ypos * 2 + 1 - core, 0).wait_send()
        for d in range(1, n_y):
            gather_copy(i, ypos, ((ypos + d) % n_y) * 2 + core, d).wait_send()
            gather_copy(i, (ypos + n_y - d) % n_y, ypos * 2 + 1 - core, n_y - 1 + d).wait_send()
            quad_copy(i, d).wait_send()
        pair_copy(i).wait_send()

    def quad_start(i):
        for d in range(1, n_y):
            quad_copy(i, d).start()

    for c in range(chunks):
        forward(c)
    for c in range(chunks):
        backward(c)
    pair_copy(1).start()
    backward_one(0)
    pair_sum(1)
    quad_start(1)
    for c in range(1, chunks):
        backward_one(c)
    g1_s[...] = g1t_s[...].T
    pair_copy(0).start()
    quad_sum(1)
    gather_start(1)
    g3_s[...] = mm(gl_s[...], h2_s[...], NT)
    pair_copy(2).start()
    pair_sum(0)
    quad_start(0)
    gather_forward(1)
    pair_sum(2)
    quad_start(2)
    quad_sum(0)
    gather_start(0)
    quad_sum(2)
    gather_start(2)
    gather_forward(0)
    gather_forward(2)
    for i in (1, 0, 2):
        gather_finish(i)
    for c in range(chunks):
        for step in range(1, n_slab):
            exchange(c, step).wait_send()


def solution(mesh):
    n_slab, n_tile = mesh.shape["slab"], mesh.shape["tile"]
    chunks = 2

    def body(
        encoded,
        spacing,
        counts,
        seg_first,
        seg_last,
        direction,
        field_in,
        field_mid,
        field_out,
        color_head,
        target,
    ):
        _, samples, rays_dev, enc = encoded.shape
        hid, out = field_out.shape[1:]
        rays = rays_dev // chunks
        total = samples * rays_dev
        f32, bf16 = jnp.float32, jnp.bfloat16
        row = lambda v: v.reshape(1, rays_dev)
        sizes = ((enc, hid), (hid, hid), (out, hid))
        any_space = pl.BlockSpec(memory_space=pl.ANY)
        vmem = pl.BlockSpec(memory_space=pltpu.VMEM)
        scratch = [
            pltpu.VMEM((chunks, samples, rays, enc), bf16),
            pltpu.VMEM((samples, rays_dev), f32),
            pltpu.VMEM((4, 1, rays_dev), jnp.int32),
            pltpu.VMEM((enc, hid), bf16),
            pltpu.VMEM((hid, hid), bf16),
            pltpu.VMEM((out, hid), bf16),
            pltpu.VMEM((3, out), f32),
            pltpu.VMEM((3, rays_dev), f32),
            pltpu.VMEM((hid, enc), bf16),
            pltpu.VMEM((hid, hid), bf16),
            pltpu.VMEM((hid, out), bf16),
            pltpu.VMEM((8, LANES), f32),
            pltpu.VMEM((LANES, 8), f32),
            pltpu.VMEM((32, hid), bf16),
            pltpu.VMEM((hid, total), bf16),
            pltpu.VMEM((hid, total), bf16),
            pltpu.VMEM((hid, total), bf16),
            pltpu.VMEM((out, total), bf16),
            pltpu.VMEM((rays // LANES, 8 * samples, LANES), f32),
            pltpu.VMEM((chunks, 6, samples, rays), f32),
            pltpu.VMEM((chunks, 1, rays), f32),
            pltpu.VMEM((chunks, 8, LANES), f32),
            pltpu.VMEM((chunks, n_slab, 8, LANES), f32),
            pltpu.VMEM((enc, hid), f32),
            pltpu.VMEM((hid, enc), f32),
            pltpu.VMEM((hid, hid), f32),
            pltpu.VMEM((out, hid), f32),
            *(pltpu.VMEM((r // 2, n), f32) for r, n in sizes),
            *(pltpu.VMEM((r // 2, n), f32) for r, n in sizes),
            *(pltpu.VMEM((n_tile // 2, r // n_tile, n), f32) for r, n in sizes),
            pltpu.SemaphoreType.DMA((chunks + 10,)),
            pltpu.SemaphoreType.DMA((chunks, n_slab)),
            pltpu.SemaphoreType.DMA((chunks, n_slab)),
            pltpu.SemaphoreType.DMA((3,)),
            pltpu.SemaphoreType.DMA((3,)),
            pltpu.SemaphoreType.DMA((3, n_tile // 2)),
            pltpu.SemaphoreType.DMA((3, n_tile // 2)),
            pltpu.SemaphoreType.DMA((3, n_tile)),
            pltpu.SemaphoreType.DMA((3, n_tile)),
        ]
        front, g1, g2, g3t = pl.pallas_call(
            functools.partial(kernel, chunks, n_slab, n_tile),
            out_shape=(
                jax.ShapeDtypeStruct((1, rays_dev), f32),
                jax.ShapeDtypeStruct((enc, hid), f32),
                jax.ShapeDtypeStruct((hid, hid), f32),
                jax.ShapeDtypeStruct((out, hid), f32),
            ),
            in_specs=[any_space] * 11,
            out_specs=(vmem,) * 4,
            scratch_shapes=scratch,
            compiler_params=pltpu.CompilerParams(
                collective_id=0, has_side_effects=True, vmem_limit_bytes=56 * 2**20
            ),
        )(
            encoded,
            spacing,
            counts,
            row(seg_first),
            row(seg_last),
            row(direction),
            field_in,
            field_mid,
            field_out.transpose(0, 2, 1),
            color_head.T,
            target.T,
        )
        return front, g1[None], g2[None], g3t.T[None]

    return jax.shard_map(
        body,
        mesh=mesh,
        in_specs=(
            P("slab", None, "tile", None),
            P("slab", None, "tile"),
            P("slab", "tile"),
            P("tile"),
            P("tile"),
            P("tile"),
            P("slab", None, None),
            P("slab", None, None),
            P("slab", None, None),
            P(),
            P("tile", None),
        ),
        out_specs=(
            P("slab", "tile"),
            P("slab", None, None),
            P("slab", None, None),
            P("slab", None, None),
        ),
        check_vma=False,
    )
```

time: 249 us -> 47.2 us (0.19); the launches traced: 246 us -> 46.9 us
  waiting for transfers between devices: 86 us -> 0 us
  other arithmetic: 49 us -> 0 us
  Pallas kernels: 0 us -> 40.3 us
  local copies, waits for them, and re-layouts: 36.5 us -> 5.97 us
  loops' own time: 22.8 us -> 0 us
  blocking collectives: 20.7 us -> 0 us
  matrix products: 16.7 us -> 0 us
  between operations: 14.4 us -> 0.64 us
    psum x1 -> x0, waiting for transfers between devices: 59.2 us -> none  [body(): lax.psum((grad_one, grad_two, grad_three), 'tile')]
    select_n x64 -> x0, other arithmetic: 40.8 us -> none  [the longest x32 40.3 us: combine(): jnp.where(front_first[:, None], color_early + trans_early[:, None] * colo...]
    pallas_call x0 -> x1, Pallas kernels: none -> 40.3 us  [body(): pl.pallas_call(functools.partial(kernel, chunks, n_slab, n_tile), out_sha...]
    all_gather x1 -> x0, waiting for transfers between devices: 26.8 us -> none  [body(): lax.all_gather(own_color[None], 'slab', axis=0, tiled=True)]
    another operation x2 -> x0, loops' own time: 22.8 us -> none  [the longest x1 11.7 us: body(): lax.scan(step_low, identity, (every_trans, every_color, slab_ids))]
    all_gather x1 -> x0, blocking collectives: 20.7 us -> none  [body(): lax.all_gather(own_trans[None], 'slab', axis=0, tiled=True)]
    dynamic_slice x32 -> x0, local copies, waits for them, and re-layouts: 20 us -> none  [body(): lax.scan(step_low, identity, (every_trans, every_color, slab_ids))]
    dot_general x9 -> x0, matrix products: 16.7 us -> none  [the longest x1 6.71 us: field_grads(): grad_one = jnp.dot(inputs.T, back_one, preferred_element_type=jnp.float32)]
  transfers between devices with their start and end apart: 2 -> 0, of which waited for: 2 -> 0; matrix products, arithmetic and copies ran while one was open for 0% -> 0% of each run, Pallas kernels for 0% -> 0%
where the time goes in v1:
time: 47.2 us; the launch traced here: 46.9 us
  Pallas kernels  40.3 us (85%)
  local copies, waits for them, and re-layouts  5.97 us (13%)
  between operations  0.64 us (1%)
    pallas_call x1, Pallas kernels, body(): pl.pallas_call(functools.partial(kernel, chunks, n_slab, n_tile), out_sha...  40.3 us
    unnamed x4, local copies, waits for them, and re-layouts  5.97 us

profile of v1, /device:TPU:1, one launch (start us, length us, event | category | flops | bytes accessed | tf_op | source)
XLA Modules:
  0.0 46.9 jit_solution(598765924154172218)
XLA Ops:
  0.6 40.3 %shard_map.138 = (f32[1,512]{1,0:T(1,128)}, f32[128,256]{1,0:T(8,128)}, f32[256,256]{1,0:T(8,128)}, f32[64,256]{1,0:T(8,128)}) custom-call(bf16[1,16,512,128]{3,2,1,0:T(8,128)(2,1)} %x_hbm.1, f32[1,16,512]{2,1,0:T(8,128)} %space_hbm.1, s32[1,512]{1,0:T(1,128)} %counts_hbm.1, s32[1,512]{1,0:T(1,128)} %bitcast.16, s32[1,512]{1,0:T(1,128)} %bitcast.17, ...), custom_call_target="tpu_custom_call" | custom-call | tf_op jit(solution)/shard_map/pallas_call | solution.py:546
  41.0 1.3 %copy.19 = f32[1,512]{1,0:T(1,128)} copy(f32[1,512]{1,0:T(1,128)} %get-tuple-element.16) | data formatting | bytes 4096
  42.2 1.6 %copy.20 = f32[1,128,256]{2,1,0:T(8,128)} copy(f32[1,128,256]{2,1,0:T(8,128)} %bitcast.12) | data formatting | bytes 262144
  43.8 1.7 %copy.21 = f32[1,256,256]{2,1,0:T(8,128)} copy(f32[1,256,256]{2,1,0:T(8,128)} %bitcast.11) | data formatting | bytes 524288
  45.5 1.5 %copy.22 = f32[1,256,64]{1,2,0:T(8,128)} copy(f32[1,256,64]{1,2,0:T(8,128)} %bitcast.13) | data formatting | bytes 131072

commit v2 on v1

v2 whole, which is shorter than its diff:
```python
import functools

import jax
import jax.numpy as jnp
from jax import lax
from jax.experimental import pallas as pl
from jax.experimental.pallas import tpu as pltpu
from jax.sharding import PartitionSpec as P

MESH = pl.DeviceIdType.MESH
NN = ((1,), (0,))
NT = ((1,), (1,))
LANES = 128


def mm(a, b, dims):
    return lax.dot_general(a, b, (dims, ((), ())), preferred_element_type=jnp.float32)


def running_sum(values):
    rows = values.shape[0]
    row_ids = lax.broadcasted_iota(jnp.int32, values.shape, 0)
    shift = 1
    while shift < rows:
        moved = pltpu.roll(values, shift, axis=0)
        values = values + jnp.where(row_ids >= shift, moved, 0.0)
        shift *= 2
    return values


def kernel(
    chunks,
    n_slab,
    n_tile,
    x_hbm,
    space_hbm,
    counts_hbm,
    first_hbm,
    last_hbm,
    dir_hbm,
    w1_hbm,
    w2_hbm,
    w3t_hbm,
    head_hbm,
    target_hbm,
    front_out,
    g1_out,
    g2_out,
    g3_out,
    x_s,
    space_s,
    ints_s,
    w1_s,
    w2_s,
    w3t_s,
    head_s,
    target_s,
    w1t_s,
    w2t_s,
    head8_s,
    headt_s,
    w3p_s,
    fold_s,
    foldt_s,
    h1_s,
    h2_s,
    b2_s,
    coef_s,
    proj_s,
    stack_s,
    saved_s,
    held_s,
    send_s,
    gather_s,
    g1_s,
    g1t_s,
    g2_s,
    g3_s,
    pair1_s,
    pair2_s,
    pair3_s,
    quad1_s,
    quad2_s,
    quad3_s,
    in_sem,
    ex_send,
    ex_recv,
    pair_send,
    pair_recv,
    quad_send,
    quad_recv,
    pass_send,
    pass_recv,
):
    samples, rays_dev = space_s.shape
    rays = rays_dev // chunks
    cols = samples * rays
    groups = rays // LANES
    me = lax.axis_index("slab")
    tile = lax.axis_index("tile")
    core, ypos = tile % 2, tile // 2
    n_y = n_tile // 2

    barrier = pltpu.get_barrier_semaphore()
    for step in range(1, n_slab):
        pl.semaphore_signal(
            barrier, inc=1, device_id={"slab": (me + step) % n_slab}, device_id_type=MESH
        )
    mates = [(ypos * 2 + 1 - core)] + [((ypos + d) % n_y) * 2 + core for d in range(1, n_y)]
    for mate in mates:
        pl.semaphore_signal(barrier, inc=1, device_id={"tile": mate}, device_id_type=MESH)

    small = [
        (w1_hbm.at[0], w1_s),
        (w2_hbm.at[0], w2_s),
        (w3t_hbm.at[0], w3t_s),
        (head_hbm, head_s),
        (space_hbm.at[0], space_s),
        (counts_hbm, ints_s.at[0]),
        (first_hbm, ints_s.at[1]),
        (last_hbm, ints_s.at[2]),
        (dir_hbm, ints_s.at[3]),
        (target_hbm, target_s),
    ]
    loads = [
        pltpu.make_async_copy(src, dst, in_sem.at[chunks + i]) for i, (src, dst) in enumerate(small)
    ]
    x_loads = [
        pltpu.make_async_copy(
            x_hbm.at[0, :, pl.ds(c * rays, rays), :], x_s.at[c], in_sem.at[c]
        )
        for c in range(chunks)
    ]
    loads[0].start()
    x_loads[0].start()
    for load in loads[1:]:
        load.start()
    for load in x_loads[1:]:
        load.start()

    loads[0].wait()
    w1t_s[...] = w1_s[...].T
    loads[1].wait()
    w2t_s[...] = w2_s[...].T
    loads[2].wait()
    loads[3].wait()
    head8_s[...] = jnp.zeros_like(head8_s)
    lane = lax.broadcasted_iota(jnp.int32, (1, LANES), 1)
    head8_s[0:1, :] = (lane == 0).astype(jnp.float32)
    head8_s[1:4, 0 : head_s.shape[1]] = head_s[...]
    headt_s[...] = head8_s[...].T
    width = w3t_s.shape[0]
    folded = lax.dot_general(
        head8_s[:, 0:width],
        w3t_s[...].astype(jnp.float32),
        (NN, ((), ())),
        precision=lax.Precision.HIGHEST,
        preferred_element_type=jnp.float32,
    )
    hi = folded.astype(jnp.bfloat16).astype(jnp.float32)
    mid = (folded - hi).astype(jnp.bfloat16).astype(jnp.float32)
    low = folded - hi - mid
    zeros = jnp.zeros_like(folded)
    w3p_s[...] = jnp.concatenate([hi, mid, low, zeros], axis=0).astype(jnp.bfloat16)
    fold_s[...] = jnp.zeros_like(fold_s)
    fold_s[0:4, :] = hi[0:4]
    fold_s[4:8, :] = hi[0:4]
    fold_s[8:12, :] = mid[0:4]
    foldt_s[...] = fold_s[...].T[:, 0:16].astype(jnp.bfloat16)
    stack_s[...] = jnp.zeros_like(stack_s)
    for load in loads[4:]:
        load.wait()

    row_ids = lax.broadcasted_iota(jnp.int32, (samples, rays), 0)
    tile_rows = lax.broadcasted_iota(jnp.int32, (8, LANES), 0)
    is_trans = (tile_rows % 4) == 0
    identity = is_trans.astype(jnp.float32)

    def spread(v):
        return jnp.where(tile_rows < 4, v[0:1, :], v[4:5, :])

    def ray_slice(c):
        return pl.ds(c * rays, rays)

    def exchange(step, source):
        return pltpu.make_async_remote_copy(
            src_ref=send_s,
            dst_ref=gather_s.at[source],
            send_sem=ex_send.at[step],
            recv_sem=ex_recv.at[source],
            device_id={"slab": (me + step) % n_slab},
            device_id_type=MESH,
        )

    def lanes_of(values, g):
        return values[:, g * LANES : (g + 1) * LANES]

    def later_sum(values, reverse):
        running = running_sum(values)
        return jnp.where(reverse, running - values, running[samples - 1 : samples, :] - running)

    def forward(c):
        x_loads[c].wait()
        x = x_s[c].reshape(cols, x_s.shape[3])
        base = c * cols
        h1 = jnp.maximum(mm(w1t_s[...], x, NT).astype(jnp.bfloat16), 0)
        h1_s[:, pl.ds(base, cols)] = h1
        h2 = jnp.maximum(mm(w2t_s[...], h1, NN).astype(jnp.bfloat16), 0)
        h2_s[:, pl.ds(base, cols)] = h2
        p = mm(w3p_s[...], h2, NN)
        p = p[0:8, :] + (p[8:16, :] + p[16:24, :])
        for j in range(samples):
            for g in range(groups):
                at = j * rays + g * LANES
                proj_s[c, g, 8 * j : 8 * j + 8, :] = p[:, at : at + LANES]
        o0, *ps = (
            jnp.concatenate(
                [proj_s[c, g, pl.ds(k, samples, stride=8), :] for g in range(groups)], 1
            )
            for k in range(4)
        )
        rs = ray_slice(c)
        counts = ints_s[0, :, rs]
        first = ints_s[1, :, rs]
        last = ints_s[2, :, rs]
        reverse = ints_s[3, :, rs] > 0
        active = (first <= me) & (me < last)
        live = ((row_ids < counts) & active).astype(jnp.float32)
        span = space_s[:, rs] * live
        soft = jnp.maximum(o0, 0.0) + jnp.log1p(jnp.exp(-jnp.abs(o0)))
        optical = soft * span
        running = running_sum(optical)
        column = running[samples - 1 : samples, :]
        before = jnp.where(reverse, column - running, running - optical)
        gone = jnp.exp(-before)
        stay = jnp.exp(-optical)
        weights = gone * (1.0 - stay)
        trans = jnp.exp(-column)
        shown = [weights * ps[k] for k in range(3)]
        rows = [trans] + [jnp.sum(shown[k], axis=0, keepdims=True) for k in range(3)]
        for g in range(groups):
            for k in range(4):
                send_s[c, 4 * g + k : 4 * g + k + 1, :] = lanes_of(rows[k], g)
        slope = span * (1.0 / (1.0 + jnp.exp(-o0)))
        spent = gone * stay
        saved_s[c, 0] = weights
        for k in range(3):
            saved_s[c, 1 + k] = slope * (spent * ps[k] - later_sum(shown[k], reverse))
        saved_s[c, 4] = -(trans * slope)

    def hold(c):
        base = c * cols
        block = 32
        for f in range(0, h2_s.shape[0], block):
            sums = [None] * 5
            for j in range(samples):
                h2 = h2_s[f : f + block, pl.ds(base + j * rays, rays)].astype(jnp.float32)
                for m in range(5):
                    term = h2 * saved_s[c, m, j : j + 1, :]
                    sums[m] = term if j == 0 else sums[m] + term
            for m in range(5):
                held_s[c, m, f : f + block, :] = sums[m]

    def compose(c):
        rs = ray_slice(c)
        rev = jnp.where(
            tile_rows < 4,
            jnp.broadcast_to(ints_s[3, :, pl.ds(c * rays, LANES)], (8, LANES)),
            jnp.broadcast_to(ints_s[3, :, pl.ds(c * rays + (groups - 1) * LANES, LANES)], (8, LANES)),
        ) > 0

        def step_of(run, item, item_first):
            run_t, item_t = spread(run), spread(item)
            run_first = jnp.where(is_trans, 0.0, run) + run_t * item
            late_first = jnp.where(is_trans, 0.0, item) + item_t * run
            return jnp.where(item_first, late_first, run_first)

        low = high = identity
        for s in range(n_slab):
            t = n_slab - 1 - s
            low = step_of(low, jnp.where(s < me, gather_s[s, c], identity), rev)
            high = step_of(high, jnp.where(t > me, gather_s[t, c], identity), jnp.logical_not(rev))
        own = send_s[c]
        front = jnp.where(rev, high, low)
        back = jnp.where(rev, low, high)
        front_t, own_t = spread(front), spread(own)
        logits = front + front_t * own + (front_t * own_t) * back
        shade = 1.0 / (1.0 + jnp.exp(-logits))
        target = jnp.zeros((8, LANES), jnp.float32)
        for g in range(groups):
            for k in range(3):
                target = jnp.where(
                    tile_rows == 4 * g + 1 + k,
                    target_s[k : k + 1, pl.ds(c * rays + g * LANES, LANES)],
                    target,
                )
        grad3 = jnp.where(is_trans, 0.0, (shade - target) * (1.0 / rays_dev) * shade * (1.0 - shade))
        seg = front_t * grad3
        dots = seg * back
        fronts, grads, seg_t = [], [[], [], []], []
        for g in range(groups):
            r = 4 * g
            fronts.append(front[r : r + 1, :])
            for k in range(3):
                grads[k].append(seg[r + 1 + k : r + 2 + k, :])
            seg_t.append(dots[r + 1 : r + 2, :] + dots[r + 2 : r + 3, :] + dots[r + 3 : r + 4, :])
        join = lambda parts: jnp.concatenate(parts, 1)
        front_out[:, rs] = join(fronts)
        return [join(grads[k]) for k in range(3)] + [join(seg_t)]

    def coefficients(c, cot):
        weights = saved_s[c, 0]
        density = (
            cot[0] * saved_s[c, 1] + cot[1] * saved_s[c, 2] + cot[2] * saved_s[c, 3] + cot[3] * saved_s[c, 4]
        )
        for m, value in enumerate([density] + [cot[k] * weights for k in range(3)]):
            hi = value.astype(jnp.bfloat16).astype(jnp.float32)
            for g in range(groups):
                for row, part in ((m, hi), (4 + m, value - hi), (8 + m, hi)):
                    stack_s[c, g, row * samples : (row + 1) * samples, :] = lanes_of(part, g)
        for j in range(samples):
            for g in range(groups):
                coef_s[:, pl.ds(c * cols + j * rays + g * LANES, LANES)] = jnp.concatenate(
                    [
                        stack_s[c, g, pl.ds(j, 8, stride=samples), :],
                        stack_s[c, g, pl.ds(8 * samples + j, 8, stride=samples), :],
                    ],
                    0,
                ).astype(jnp.bfloat16)

    def grad_out(cots):
        hid = h2_s.shape[0]
        block = 32
        column = lax.broadcasted_iota(jnp.int32, (block, LANES), 1)
        for f in range(0, hid, block):
            parts = [0.0] * 4
            for c in range(chunks):
                for g in range(groups):
                    at = pl.ds(g * LANES, LANES)
                    shown = held_s[c, 0, f : f + block, at]
                    for k in range(3):
                        parts[k] = parts[k] + shown * lanes_of(cots[c][k], g)
                    for m in range(4):
                        parts[3] = parts[3] + held_s[c, 1 + m, f : f + block, at] * lanes_of(cots[c][m], g)
            packed = jnp.zeros((block, LANES), jnp.float32)
            for k in range(4):
                packed = jnp.where(column == k, jnp.sum(parts[k], axis=1, keepdims=True), packed)
            held_s[0, 0, f : f + block, 0:LANES] = packed
        sums = held_s[0, 0, :, 0:LANES].T
        first_row = lax.broadcasted_iota(jnp.int32, (width, 1), 0) == 0
        total = jnp.where(first_row, sums[3:4, :], 0.0)
        for k in range(3):
            total = total + headt_s[0:width, 1 + k : 2 + k] * sums[k : k + 1, :]
        g3_s[...] = total

    def backward_two(c):
        base = c * cols
        b2 = mm(foldt_s[...], coef_s[:, pl.ds(base, cols)], NN).astype(jnp.bfloat16)
        b2 = jnp.where(h2_s[:, pl.ds(base, cols)] > 0, b2, 0)
        b2_s[:, pl.ds(base, cols)] = b2
        part = mm(h1_s[:, pl.ds(base, cols)], b2, NT)
        g2_s[...] = part if c == 0 else g2_s[...] + part

    def backward_one(c):
        base = c * cols
        b1 = mm(w2_s[...], b2_s[:, pl.ds(base, cols)], NN).astype(jnp.bfloat16)
        b1 = jnp.where(h1_s[:, pl.ds(base, cols)] > 0, b1, 0)
        part = mm(b1, x_s[c].reshape(cols, x_s.shape[3]), NN)
        g1t_s[...] = part if c == 0 else g1t_s[...] + part

    grads = (
        (g1_s, pair1_s, quad1_s, g1_out),
        (g2_s, pair2_s, quad2_s, g2_out),
        (g3_s, pair3_s, quad3_s, g3_out),
    )
    partner = ypos * 2 + 1 - core

    def half_rows(i, k):
        rows = grads[i][1].shape[0]
        return pl.ds(pl.multiple_of(k * rows, 8), rows)

    def pair_copy(i):
        whole, pair = grads[i][:2]
        return pltpu.make_async_remote_copy(
            src_ref=whole.at[half_rows(i, 1 - core), :],
            dst_ref=pair,
            send_sem=pair_send.at[i],
            recv_sem=pair_recv.at[i],
            device_id={"tile": partner},
            device_id_type=MESH,
        )

    def quad_copy(i, d, source):
        quad = grads[i][2]
        return pltpu.make_async_remote_copy(
            src_ref=quad.at[ypos],
            dst_ref=quad.at[source],
            send_sem=quad_send.at[i, d],
            recv_sem=quad_recv.at[i, source],
            device_id={"tile": ((ypos + d) % n_y) * 2 + core},
            device_id_type=MESH,
        )

    def pass_copy(i, k):
        out = grads[i][3]
        at = half_rows(i, k)
        return pltpu.make_async_remote_copy(
            src_ref=out.at[at, :],
            dst_ref=out.at[at, :],
            send_sem=pass_send.at[i],
            recv_sem=pass_recv.at[i],
            device_id={"tile": partner},
            device_id_type=MESH,
        )

    def spread_half(i):
        whole, pair, quad = grads[i][:3]
        pair_copy(i).wait_recv()
        quad[ypos] = whole[half_rows(i, core), :] + pair[...]
        for d in range(1, n_y):
            quad_copy(i, d, ypos).start()

    def finish_half(i):
        quad, out = grads[i][2:]
        for d in range(1, n_y):
            quad_copy(i, d, (ypos + n_y - d) % n_y).wait_recv()
        total = quad[0]
        for y in range(1, n_y):
            total = total + quad[y]
        out[half_rows(i, core), :] = total
        pass_copy(i, core).start()

    for c in range(chunks):
        forward(c)
    pl.semaphore_wait(barrier, n_slab - 1 + len(mates))
    for step in range(1, n_slab):
        exchange(step, me).start()
    gather_s[me] = send_s[...]
    for c in range(chunks):
        hold(c)
    for step in range(1, n_slab):
        exchange(step, (me + n_slab - step) % n_slab).wait_recv()
    cots = [compose(c) for c in range(chunks)]
    for c in range(chunks):
        coefficients(c, cots[c])
    grad_out(cots)
    pair_copy(2).start()
    backward_two(0)
    spread_half(2)
    for c in range(1, chunks):
        backward_two(c)
    pair_copy(1).start()
    backward_one(0)
    spread_half(1)
    for c in range(1, chunks):
        backward_one(c)
    g1_s[...] = g1t_s[...].T
    pair_copy(0).start()
    finish_half(2)
    spread_half(0)
    finish_half(1)
    finish_half(0)
    for i in (2, 1, 0):
        pass_copy(i, 1 - core).wait_recv()
    for i in (2, 1, 0):
        pass_copy(i, core).wait_send()
        pair_copy(i).wait_send()
        for d in range(1, n_y):
            quad_copy(i, d, ypos).wait_send()
    for step in range(1, n_slab):
        exchange(step, me).wait_send()


def hand_on(*refs):
    half = len(refs) // 2
    sem = refs[-1]
    copies = [
        pltpu.make_async_copy(src, dst, sem.at[i])
        for i, (src, dst) in enumerate(zip(refs[:half], refs[half : 2 * half]))
    ]
    for copy in copies:
        copy.start()
    for copy in copies:
        copy.wait()


def solution(mesh):
    n_slab, n_tile = mesh.shape["slab"], mesh.shape["tile"]
    chunks = 2

    def body(
        encoded,
        spacing,
        counts,
        seg_first,
        seg_last,
        direction,
        field_in,
        field_mid,
        field_out,
        color_head,
        target,
    ):
        _, samples, rays_dev, enc = encoded.shape
        hid, out = field_out.shape[1:]
        rays = rays_dev // chunks
        total = samples * rays_dev
        f32, bf16 = jnp.float32, jnp.bfloat16
        row = lambda v: v.reshape(1, rays_dev)
        sizes = ((enc, hid), (hid, hid), (out, hid))
        any_space = pl.BlockSpec(memory_space=pl.ANY)
        vmem = pl.BlockSpec(memory_space=pltpu.VMEM)
        scratch = [
            pltpu.VMEM((chunks, samples, rays, enc), bf16),
            pltpu.VMEM((samples, rays_dev), f32),
            pltpu.VMEM((4, 1, rays_dev), jnp.int32),
            pltpu.VMEM((enc, hid), bf16),
            pltpu.VMEM((hid, hid), bf16),
            pltpu.VMEM((out, hid), bf16),
            pltpu.VMEM((3, out), f32),
            pltpu.VMEM((3, rays_dev), f32),
            pltpu.VMEM((hid, enc), bf16),
            pltpu.VMEM((hid, hid), bf16),
            pltpu.VMEM((8, LANES), f32),
            pltpu.VMEM((LANES, 8), f32),
            pltpu.VMEM((32, hid), bf16),
            pltpu.VMEM((LANES, hid), f32),
            pltpu.VMEM((hid, 16), bf16),
            pltpu.VMEM((hid, total), bf16),
            pltpu.VMEM((hid, total), bf16),
            pltpu.VMEM((hid, total), bf16),
            pltpu.VMEM((16, total), bf16),
            pltpu.VMEM((chunks, rays // LANES, 8 * samples, LANES), f32),
            pltpu.VMEM((chunks, rays // LANES, 16 * samples, LANES), f32),
            pltpu.VMEM((chunks, 5, samples, rays), f32),
            pltpu.VMEM((chunks, 5, hid, rays), f32),
            pltpu.VMEM((chunks, 8, LANES), f32),
            pltpu.VMEM((n_slab, chunks, 8, LANES), f32),
            pltpu.VMEM((enc, hid), f32),
            pltpu.VMEM((hid, enc), f32),
            pltpu.VMEM((hid, hid), f32),
            pltpu.VMEM((out, hid), f32),
            *(pltpu.VMEM((r // 2, n), f32) for r, n in sizes),
            *(pltpu.VMEM((n_tile // 2, r // 2, n), f32) for r, n in sizes),
            pltpu.SemaphoreType.DMA((chunks + 10,)),
            pltpu.SemaphoreType.DMA((n_slab,)),
            pltpu.SemaphoreType.DMA((n_slab,)),
            pltpu.SemaphoreType.DMA((3,)),
            pltpu.SemaphoreType.DMA((3,)),
            pltpu.SemaphoreType.DMA((3, n_tile // 2)),
            pltpu.SemaphoreType.DMA((3, n_tile // 2)),
            pltpu.SemaphoreType.DMA((3,)),
            pltpu.SemaphoreType.DMA((3,)),
        ]
        shapes = (
            jax.ShapeDtypeStruct((1, rays_dev), f32),
            jax.ShapeDtypeStruct((enc, hid), f32),
            jax.ShapeDtypeStruct((hid, hid), f32),
            jax.ShapeDtypeStruct((out, hid), f32),
        )
        results = pl.pallas_call(
            functools.partial(kernel, chunks, n_slab, n_tile),
            out_shape=shapes,
            in_specs=[any_space] * 11,
            out_specs=(vmem,) * 4,
            scratch_shapes=scratch,
            compiler_params=pltpu.CompilerParams(
                collective_id=0, has_side_effects=True, vmem_limit_bytes=56 * 2**20
            ),
        )(
            encoded,
            spacing,
            counts,
            row(seg_first),
            row(seg_last),
            row(direction),
            field_in,
            field_mid,
            field_out.transpose(0, 2, 1),
            color_head.T,
            target.T,
        )
        front, g1, g2, g3t = pl.pallas_call(
            hand_on,
            out_shape=shapes,
            in_specs=[any_space] * 4,
            out_specs=(any_space,) * 4,
            scratch_shapes=[pltpu.SemaphoreType.DMA((4,))],
        )(*results)
        return front, g1[None], g2[None], g3t.T[None]

    return jax.shard_map(
        body,
        mesh=mesh,
        in_specs=(
            P("slab", None, "tile", None),
            P("slab", None, "tile"),
            P("slab", "tile"),
            P("tile"),
            P("tile"),
            P("tile"),
            P("slab", None, None),
            P("slab", None, None),
            P("slab", None, None),
            P(),
            P("tile", None),
        ),
        out_specs=(
            P("slab", "tile"),
            P("slab", None, None),
            P("slab", None, None),
            P("slab", None, None),
        ),
        check_vma=False,
    )
```

time: 47.2 us -> 51.1 us (1.083)
  Pallas kernels: 40.3 us -> 50.4 us
  local copies, waits for them, and re-layouts: 5.97 us -> 0 us
    pallas_call x0 -> x1, Pallas kernels: none -> 15.1 us  [body(): pl.pallas_call(hand_on, out_shape=shapes, in_specs=[any_space] * 4, out_s...]
    unnamed x4 -> x0, local copies, waits for them, and re-layouts: 5.97 us -> none
    pallas_call x1, Pallas kernels: 40.3 us -> 35.3 us  [body(): pl.pallas_call(functools.partial(kernel, chunks, n_slab, n_tile), out_sha...]
where the time goes in v2:
time: 51.1 us; the launch traced here: 51 us
  Pallas kernels  50.4 us (99%)
  between operations  0.64 us (1%)
    pallas_call x1, Pallas kernels, body(): pl.pallas_call(functools.partial(kernel, chunks, n_slab, n_tile), out_sha...  35.3 us
    pallas_call x1, Pallas kernels, body(): pl.pallas_call(hand_on, out_shape=shapes, in_specs=[any_space] * 4, out_s...  15.1 us

profile of v2, /device:TPU:1, one launch (start us, length us, event | category | flops | bytes accessed | tf_op | source)
XLA Modules:
  0.0 51.0 jit_solution(15146762650829467006)
XLA Ops:
  0.6 35.3 %shard_map.138 = (f32[1,512]{1,0:T(1,128)}, f32[128,256]{1,0:T(8,128)}, f32[256,256]{1,0:T(8,128)}, f32[64,256]{1,0:T(8,128)}) custom-call(bf16[1,16,512,128]{3,2,1,0:T(8,128)(2,1)} %x_hbm.1, f32[1,16,512]{2,1,0:T(8,128)} %space_hbm.1, s32[1,512]{1,0:T(1,128)} %counts_hbm.1, s32[1,512]{1,0:T(1,128)} %bitcast.13, s32[1,512]{1,0:T(1,128)} %bitcast.14, ...), custom_call_target="tpu_custom_call" | custom-call | tf_op jit(solution)/shard_map/pallas_call | solution.py:561
  35.9 15.1 %shard_map.139 = (f32[1,512]{1,0:T(1,128)}, f32[128,256]{1,0:T(8,128)}, f32[256,256]{1,0:T(8,128)}, f32[64,256]{1,0:T(8,128)}) custom-call(f32[1,512]{1,0:T(1,128)} %get-tuple-element.12.refs_0_, f32[128,256]{1,0:T(8,128)} %get-tuple-element.13.refs_1_, f32[256,256]{1,0:T(8,128)} %get-tuple-element.14.refs_2_, f32[64,256]{1,0:T(8,128)} %get-tuple-element.15.refs_3_), custom_call_target="tpu_custom_call" | custom-call | tf_op jit(solution)/shard_map/pallas_call | solution.py:583

commit v3 on v2

--- a/solution.py
+++ b/solution.py
@@ -473,15 +473,8 @@
 
 def hand_on(*refs):
     half = len(refs) // 2
-    sem = refs[-1]
-    copies = [
-        pltpu.make_async_copy(src, dst, sem.at[i])
-        for i, (src, dst) in enumerate(zip(refs[:half], refs[half : 2 * half]))
-    ]
-    for copy in copies:
-        copy.start()
-    for copy in copies:
-        copy.wait()
+    for src, dst in zip(refs[:half], refs[half:]):
+        dst[...] = src[...]
 
 
 def solution(mesh):
@@ -583,9 +576,8 @@
         front, g1, g2, g3t = pl.pallas_call(
             hand_on,
             out_shape=shapes,
-            in_specs=[any_space] * 4,
-            out_specs=(any_space,) * 4,
-            scratch_shapes=[pltpu.SemaphoreType.DMA((4,))],
+            in_specs=[vmem] * 4,
+            out_specs=(vmem,) * 4,
         )(*results)
         return front, g1[None], g2[None], g3t.T[None]
 

time: 51.1 us -> 37.9 us (0.74)
  Pallas kernels: 50.4 us -> 37.1 us
    pallas_call x1, Pallas kernels: 15.1 us -> 1.8 us  [body(): pl.pallas_call(hand_on, out_shape=shapes, in_specs=[vmem] * 4, out_specs=...]
where the time goes in v3:
time: 37.9 us; the launch traced here: 37.7 us
  Pallas kernels  37.1 us (98%)
  between operations  0.64 us (2%)
    pallas_call x1, Pallas kernels, body(): pl.pallas_call(functools.partial(kernel, chunks, n_slab, n_tile), out_sha...  35.3 us
    pallas_call x1, Pallas kernels, body(): pl.pallas_call(hand_on, out_shape=shapes, in_specs=[vmem] * 4, out_specs=...  1.8 us

profile of v3, /device:TPU:1, one launch (start us, length us, event | category | flops | bytes accessed | tf_op | source)
XLA Modules:
  0.0 37.7 jit_solution(15305143382137970665)
XLA Ops:
  0.6 35.3 %shard_map.138 = (f32[1,512]{1,0:T(1,128)}, f32[128,256]{1,0:T(8,128)}, f32[256,256]{1,0:T(8,128)}, f32[64,256]{1,0:T(8,128)}) custom-call(bf16[1,16,512,128]{3,2,1,0:T(8,128)(2,1)} %x_hbm.1, f32[1,16,512]{2,1,0:T(8,128)} %space_hbm.1, s32[1,512]{1,0:T(1,128)} %counts_hbm.1, s32[1,512]{1,0:T(1,128)} %bitcast.13, s32[1,512]{1,0:T(1,128)} %bitcast.14, ...), custom_call_target="tpu_custom_call" | custom-call | tf_op jit(solution)/shard_map/pallas_call | solution.py:554
  35.9 1.8 %shard_map.139 = (f32[1,512]{1,0:T(1,128)}, f32[128,256]{1,0:T(8,128)}, f32[256,256]{1,0:T(8,128)}, f32[64,256]{1,0:T(8,128)}) custom-call(f32[1,512]{1,0:T(1,128)} %get-tuple-element.12.refs_0_, f32[128,256]{1,0:T(8,128)} %get-tuple-element.13.refs_1_, f32[256,256]{1,0:T(8,128)} %get-tuple-element.14.refs_2_, f32[64,256]{1,0:T(8,128)} %get-tuple-element.15.refs_3_), custom_call_target="tpu_custom_call" | custom-call | tf_op jit(solution)/shard_map/pallas_call | solution.py:576

commit v4 on v3

--- a/solution.py
+++ b/solution.py
@@ -79,16 +79,25 @@
     pair1_s,
     pair2_s,
     pair3_s,
-    quad1_s,
-    quad2_s,
-    quad3_s,
+    half1_s,
+    half2_s,
+    half3_s,
+    mid1_s,
+    mid2_s,
+    mid3_s,
+    near1_s,
+    near2_s,
+    near3_s,
+    far1_s,
+    far2_s,
+    far3_s,
     in_sem,
     ex_send,
     ex_recv,
     pair_send,
     pair_recv,
-    quad_send,
-    quad_recv,
+    swap_send,
+    swap_recv,
     pass_send,
     pass_recv,
 ):
@@ -106,7 +115,8 @@
         pl.semaphore_signal(
             barrier, inc=1, device_id={"slab": (me + step) % n_slab}, device_id_type=MESH
         )
-    mates = [(ypos * 2 + 1 - core)] + [((ypos + d) % n_y) * 2 + core for d in range(1, n_y)]
+    across = (ypos + 1 - 2 * (ypos % 2), n_y - 1 - ypos)
+    mates = [ypos * 2 + 1 - core] + [y * 2 + core for y in across]
     for mate in mates:
         pl.semaphore_signal(barrier, inc=1, device_id={"tile": mate}, device_id_type=MESH)
 
@@ -369,9 +379,9 @@
         g1t_s[...] = part if c == 0 else g1t_s[...] + part
 
     grads = (
-        (g1_s, pair1_s, quad1_s, g1_out),
-        (g2_s, pair2_s, quad2_s, g2_out),
-        (g3_s, pair3_s, quad3_s, g3_out),
+        (g1_s, pair1_s, half1_s, near1_s, mid1_s, far1_s, g1_out),
+        (g2_s, pair2_s, half2_s, near2_s, mid2_s, far2_s, g2_out),
+        (g3_s, pair3_s, half3_s, near3_s, mid3_s, far3_s, g3_out),
     )
     partner = ypos * 2 + 1 - core
 
@@ -390,19 +400,21 @@
             device_id_type=MESH,
         )
 
-    def quad_copy(i, d, source):
-        quad = grads[i][2]
+    def swap_copy(i, stage, part):
+        source, target = (grads[i][2:4], grads[i][4:6])[stage]
+        rows = source.shape[0] // 2
+        at = pl.ds(part * rows, rows)
         return pltpu.make_async_remote_copy(
-            src_ref=quad.at[ypos],
-            dst_ref=quad.at[source],
-            send_sem=quad_send.at[i, d],
-            recv_sem=quad_recv.at[i, source],
-            device_id={"tile": ((ypos + d) % n_y) * 2 + core},
+            src_ref=source.at[at, :],
+            dst_ref=target.at[at, :],
+            send_sem=swap_send.at[i, stage, part],
+            recv_sem=swap_recv.at[i, stage, part],
+            device_id={"tile": across[(stage + part) % 2] * 2 + core},
             device_id_type=MESH,
         )
 
     def pass_copy(i, k):
-        out = grads[i][3]
+        out = grads[i][6]
         at = half_rows(i, k)
         return pltpu.make_async_remote_copy(
             src_ref=out.at[at, :],
@@ -413,21 +425,27 @@
             device_id_type=MESH,
         )
 
-    def spread_half(i):
-        whole, pair, quad = grads[i][:3]
+    def swap_first(i):
+        whole, pair, half = grads[i][:3]
         pair_copy(i).wait_recv()
-        quad[ypos] = whole[half_rows(i, core), :] + pair[...]
-        for d in range(1, n_y):
-            quad_copy(i, d, ypos).start()
+        half[...] = whole[half_rows(i, core), :] + pair[...]
+        for part in range(2):
+            swap_copy(i, 0, part).start()
+
+    def swap_second(i):
+        half, near, mid = grads[i][2:5]
+        rows = half.shape[0] // 2
+        for part in range(2):
+            swap_copy(i, 0, part).wait_recv()
+            at = slice(part * rows, (part + 1) * rows)
+            mid[at, :] = half[at, :] + near[at, :]
+            swap_copy(i, 1, part).start()
 
     def finish_half(i):
-        quad, out = grads[i][2:]
-        for d in range(1, n_y):
-            quad_copy(i, d, (ypos + n_y - d) % n_y).wait_recv()
-        total = quad[0]
-        for y in range(1, n_y):
-            total = total + quad[y]
-        out[half_rows(i, core), :] = total
+        mid, far, out = grads[i][4:]
+        for part in range(2):
+            swap_copy(i, 1, part).wait_recv()
+        out[half_rows(i, core), :] = mid[...] + far[...]
         pass_copy(i, core).start()
 
     for c in range(chunks):
@@ -446,18 +464,21 @@
     grad_out(cots)
     pair_copy(2).start()
     backward_two(0)
-    spread_half(2)
+    swap_first(2)
     for c in range(1, chunks):
         backward_two(c)
     pair_copy(1).start()
     backward_one(0)
-    spread_half(1)
+    swap_first(1)
     for c in range(1, chunks):
         backward_one(c)
     g1_s[...] = g1t_s[...].T
     pair_copy(0).start()
+    swap_second(2)
+    swap_first(0)
+    swap_second(1)
     finish_half(2)
-    spread_half(0)
+    swap_second(0)
     finish_half(1)
     finish_half(0)
     for i in (2, 1, 0):
@@ -465,8 +486,9 @@
     for i in (2, 1, 0):
         pass_copy(i, core).wait_send()
         pair_copy(i).wait_send()
-        for d in range(1, n_y):
-            quad_copy(i, d, ypos).wait_send()
+        for stage in range(2):
+            for part in range(2):
+                swap_copy(i, stage, part).wait_send()
     for step in range(1, n_slab):
         exchange(step, me).wait_send()
 
@@ -534,14 +556,17 @@
             pltpu.VMEM((hid, hid), f32),
             pltpu.VMEM((out, hid), f32),
             *(pltpu.VMEM((r // 2, n), f32) for r, n in sizes),
-            *(pltpu.VMEM((n_tile // 2, r // 2, n), f32) for r, n in sizes),
+            *(pltpu.VMEM((r // 2, n), f32) for r, n in sizes),
+            *(pltpu.VMEM((r // 2, n), f32) for r, n in sizes),
+            *(pltpu.VMEM((r // 2, n), f32) for r, n in sizes),
+            *(pltpu.VMEM((r // 2, n), f32) for r, n in sizes),
             pltpu.SemaphoreType.DMA((chunks + 10,)),
             pltpu.SemaphoreType.DMA((n_slab,)),
             pltpu.SemaphoreType.DMA((n_slab,)),
             pltpu.SemaphoreType.DMA((3,)),
             pltpu.SemaphoreType.DMA((3,)),
-            pltpu.SemaphoreType.DMA((3, n_tile // 2)),
-            pltpu.SemaphoreType.DMA((3, n_tile // 2)),
+            pltpu.SemaphoreType.DMA((3, 2, 2)),
+            pltpu.SemaphoreType.DMA((3, 2, 2)),
             pltpu.SemaphoreType.DMA((3,)),
             pltpu.SemaphoreType.DMA((3,)),
         ]
@@ -553,7 +578,7 @@
         )
         results = pl.pallas_call(
             functools.partial(kernel, chunks, n_slab, n_tile),
-            out_shape=shapes,
+            out_shape=tuple(pltpu.VMEM(q.shape, q.dtype) for q in shapes),
             in_specs=[any_space] * 11,
             out_specs=(vmem,) * 4,
             scratch_shapes=scratch,
@@ -578,7 +603,7 @@
             out_shape=shapes,
             in_specs=[vmem] * 4,
             out_specs=(vmem,) * 4,
-        )(*results)
+        )(*(pltpu.with_memory_space_constraint(r, pltpu.VMEM) for r in results))
         return front, g1[None], g2[None], g3t.T[None]
 
     return jax.shard_map(

time: 37.9 us -> 33.3 us (0.88)
  Pallas kernels: 37.1 us -> 32.5 us
    pallas_call x1, Pallas kernels: 35.3 us -> 31.7 us  [body(): pl.pallas_call(functools.partial(kernel, chunks, n_slab, n_tile), out_sha...]
    pallas_call x1, Pallas kernels: 1.8 us -> 0.79 us  [body(): pl.pallas_call(hand_on, out_shape=shapes, in_specs=[vmem] * 4, out_specs=...]
where the time goes in v4:
time: 33.3 us; the launch traced here: 33.1 us
  Pallas kernels  32.5 us (98%)
  between operations  0.64 us (2%)
    pallas_call x1, Pallas kernels, body(): pl.pallas_call(functools.partial(kernel, chunks, n_slab, n_tile), out_sha...  31.7 us
    pallas_call x1, Pallas kernels, body(): pl.pallas_call(hand_on, out_shape=shapes, in_specs=[vmem] * 4, out_specs=...  0.79 us

profile of v4, /device:TPU:1, one launch (start us, length us, event | category | flops | bytes accessed | tf_op | source)
XLA Modules:
  0.0 33.1 jit_solution(15028422140319056558)
XLA Ops:
  0.6 31.7 %shard_map.138 = (f32[1,512]{1,0:T(1,128)S(1)}, f32[128,256]{1,0:T(8,128)S(1)}, f32[256,256]{1,0:T(8,128)S(1)}, f32[64,256]{1,0:T(8,128)S(1)}) custom-call(bf16[1,16,512,128]{3,2,1,0:T(8,128)(2,1)} %x_hbm.1, f32[1,16,512]{2,1,0:T(8,128)} %space_hbm.1, s32[1,512]{1,0:T(1,128)} %counts_hbm.1, s32[1,512]{1,0:T(1,128)} %bitcast.13, s32[1,512]{1,0:T(1,128)} %bitcast.14, ...), custom_call_target="tpu_custom_call" | custom-call | tf_op jit(solution)/shard_map/pallas_call | solution.py:579
  32.3 0.8 %shard_map.139 = (f32[1,512]{1,0:T(1,128)}, f32[128,256]{1,0:T(8,128)}, f32[256,256]{1,0:T(8,128)}, f32[64,256]{1,0:T(8,128)}) custom-call(f32[1,512]{1,0:T(1,128)S(1)} %get-tuple-element.12.refs_0_, f32[128,256]{1,0:T(8,128)S(1)} %get-tuple-element.13.refs_1_, f32[256,256]{1,0:T(8,128)S(1)} %get-tuple-element.14.refs_2_, ...), custom_call_target="tpu_custom_call" | custom-call | tf_op jit(solution)/shard_map/pallas_call | solution.py:601

commit v5 on v4

--- a/solution.py
+++ b/solution.py
@@ -1,4 +1,5 @@
 import functools
+import math
 
 import jax
 import jax.numpy as jnp
@@ -79,9 +80,6 @@
     pair1_s,
     pair2_s,
     pair3_s,
-    half1_s,
-    half2_s,
-    half3_s,
     mid1_s,
     mid2_s,
     mid3_s,
@@ -91,6 +89,9 @@
     far1_s,
     far2_s,
     far3_s,
+    other1_s,
+    other3_s,
+    half2_s,
     in_sem,
     ex_send,
     ex_recv,
@@ -116,7 +117,7 @@
             barrier, inc=1, device_id={"slab": (me + step) % n_slab}, device_id_type=MESH
         )
     across = (ypos + 1 - 2 * (ypos % 2), n_y - 1 - ypos)
-    mates = [ypos * 2 + 1 - core] + [y * 2 + core for y in across]
+    mates = [ypos * 2 + 1 - core] + [y * 2 + c for y in across for c in (core, 1 - core)]
     for mate in mates:
         pl.semaphore_signal(barrier, inc=1, device_id={"tile": mate}, device_id_type=MESH)
 
@@ -192,15 +193,29 @@
     def ray_slice(c):
         return pl.ds(c * rays, rays)
 
+    side = math.isqrt(n_slab)
+    near = lambda d: min(d, side - d)
+    moves = sorted(
+        ((dx, dz) for dx in range(side) for dz in range(side) if dx or dz),
+        key=lambda d: -near(d[0]) - near(d[1]),
+    )
+
+    def slab_at(dx, dz):
+        return (me // side + dx) % side * side + (me % side + dz) % side
+
     def exchange(step, source):
         return pltpu.make_async_remote_copy(
             src_ref=send_s,
             dst_ref=gather_s.at[source],
             send_sem=ex_send.at[step],
             recv_sem=ex_recv.at[source],
-            device_id={"slab": (me + step) % n_slab},
+            device_id={"slab": slab_at(*moves[step])},
             device_id_type=MESH,
         )
+
+    def origin(step):
+        dx, dz = moves[step]
+        return slab_at(side - dx, side - dz)
 
     def lanes_of(values, g):
         return values[:, g * LANES : (g + 1) * LANES]
@@ -209,7 +224,7 @@
         running = running_sum(values)
         return jnp.where(reverse, running - values, running[samples - 1 : samples, :] - running)
 
-    def forward(c):
+    def forward_samples(c):
         x_loads[c].wait()
         x = x_s[c].reshape(cols, x_s.shape[3])
         base = c * cols
@@ -223,6 +238,8 @@
             for g in range(groups):
                 at = j * rays + g * LANES
                 proj_s[c, g, 8 * j : 8 * j + 8, :] = p[:, at : at + LANES]
+
+    def forward_rays(c):
         o0, *ps = (
             jnp.concatenate(
                 [proj_s[c, g, pl.ds(k, samples, stride=8), :] for g in range(groups)], 1
@@ -251,8 +268,11 @@
         for g in range(groups):
             for k in range(4):
                 send_s[c, 4 * g + k : 4 * g + k + 1, :] = lanes_of(rows[k], g)
+        return o0, ps, span, gone * stay, weights, shown, trans, reverse
+
+    def slopes(c, values):
+        o0, ps, span, spent, weights, shown, trans, reverse = values
         slope = span * (1.0 / (1.0 + jnp.exp(-o0)))
-        spent = gone * stay
         saved_s[c, 0] = weights
         for k in range(3):
             saved_s[c, 1 + k] = slope * (spent * ps[k] - later_sum(shown[k], reverse))
@@ -379,15 +399,19 @@
         g1t_s[...] = part if c == 0 else g1t_s[...] + part
 
     grads = (
-        (g1_s, pair1_s, half1_s, near1_s, mid1_s, far1_s, g1_out),
-        (g2_s, pair2_s, half2_s, near2_s, mid2_s, far2_s, g2_out),
-        (g3_s, pair3_s, half3_s, near3_s, mid3_s, far3_s, g3_out),
+        (g1_s, pair1_s, near1_s, mid1_s, far1_s, other1_s, g1_out),
+        (g2_s, pair2_s, near2_s, mid2_s, far2_s, None, g2_out),
+        (g3_s, pair3_s, near3_s, mid3_s, far3_s, other3_s, g3_out),
     )
     partner = ypos * 2 + 1 - core
 
     def half_rows(i, k):
         rows = grads[i][1].shape[0]
         return pl.ds(pl.multiple_of(k * rows, 8), rows)
+
+    def part_rows(i, part):
+        rows = grads[i][1].shape[0] // 2
+        return pl.ds(part * rows, rows)
 
     def pair_copy(i):
         whole, pair = grads[i][:2]
@@ -400,96 +424,128 @@
             device_id_type=MESH,
         )
 
-    def swap_copy(i, stage, part):
-        source, target = (grads[i][2:4], grads[i][4:6])[stage]
-        rows = source.shape[0] // 2
-        at = pl.ds(part * rows, rows)
+    def swap_copy(i, stage, part, turn):
+        whole, pair, near, mid, far = grads[i][:5]
+        rows = pair.shape[0] // 2
+        if stage == 0 and i == 1:
+            source, target = half2_s.at[part_rows(i, part), :], near
+        elif stage == 0:
+            half = 1 - core if turn else core
+            at = pl.multiple_of(half * (2 * rows) + part * rows, 8)
+            source, target = whole.at[pl.ds(at, rows), :], near
+        else:
+            source, target = mid.at[part_rows(i, part), :], far
         return pltpu.make_async_remote_copy(
-            src_ref=source.at[at, :],
-            dst_ref=target.at[at, :],
-            send_sem=swap_send.at[i, stage, part],
-            recv_sem=swap_recv.at[i, stage, part],
-            device_id={"tile": across[(stage + part) % 2] * 2 + core},
+            src_ref=source,
+            dst_ref=target.at[turn, part_rows(i, part), :],
+            send_sem=swap_send.at[i, stage, part, turn],
+            recv_sem=swap_recv.at[i, stage, part, turn],
+            device_id={"tile": across[(stage + part) % 2] * 2 + (1 - core if turn else core)},
             device_id_type=MESH,
         )
 
-    def pass_copy(i, k):
-        out = grads[i][6]
-        at = half_rows(i, k)
+    def pass_copy(i):
+        source, target = grads[i][3], grads[i][5]
+        if i == 1:
+            source = target = g2_out.at[half_rows(1, core), :]
         return pltpu.make_async_remote_copy(
-            src_ref=out.at[at, :],
-            dst_ref=out.at[at, :],
+            src_ref=source,
+            dst_ref=target,
             send_sem=pass_send.at[i],
             recv_sem=pass_recv.at[i],
             device_id={"tile": partner},
             device_id_type=MESH,
         )
 
-    def swap_first(i):
-        whole, pair, half = grads[i][:3]
+    def send_own(i):
+        for turn in range(2):
+            for part in range(2):
+                swap_copy(i, 0, part, turn).start()
+        pair_copy(i).start()
+
+    def send_sums(i):
+        whole, pair, near, mid = grads[i][:4]
+        rows = pair.shape[0] // 2
         pair_copy(i).wait_recv()
-        half[...] = whole[half_rows(i, core), :] + pair[...]
         for part in range(2):
-            swap_copy(i, 0, part).start()
-
-    def swap_second(i):
-        half, near, mid = grads[i][2:5]
-        rows = half.shape[0] // 2
+            for turn in range(2):
+                swap_copy(i, 0, part, turn).wait_recv()
+            at = part_rows(i, part)
+            own = whole[pl.ds(pl.multiple_of(core * (2 * rows) + part * rows, 8), rows), :]
+            mid[at, :] = (own + pair[at, :]) + (near[0, at, :] + near[1, at, :])
+            for turn in range(2):
+                swap_copy(i, 1, part, turn).start()
+        pass_copy(i).start()
+
+    def lean_first():
+        pair_copy(1).wait_recv()
+        half2_s[...] = g2_s[half_rows(1, core), :] + pair2_s[...]
         for part in range(2):
-            swap_copy(i, 0, part).wait_recv()
-            at = slice(part * rows, (part + 1) * rows)
-            mid[at, :] = half[at, :] + near[at, :]
-            swap_copy(i, 1, part).start()
-
-    def finish_half(i):
-        mid, far, out = grads[i][4:]
+            swap_copy(1, 0, part, 0).start()
+
+    def lean_second():
         for part in range(2):
-            swap_copy(i, 1, part).wait_recv()
-        out[half_rows(i, core), :] = mid[...] + far[...]
-        pass_copy(i, core).start()
+            swap_copy(1, 0, part, 0).wait_recv()
+            at = part_rows(1, part)
+            mid2_s[at, :] = half2_s[at, :] + near2_s[0, at, :]
+            swap_copy(1, 1, part, 0).start()
+
+    def lean_third():
+        for part in range(2):
+            swap_copy(1, 1, part, 0).wait_recv()
+        g2_out[half_rows(1, core), :] = mid2_s[...] + far2_s[0]
+        pass_copy(1).start()
+
+    def finish(i):
+        mid, far, other, out = grads[i][3:]
+        for turn in range(2):
+            for part in range(2):
+                swap_copy(i, 1, part, turn).wait_recv()
+        out[half_rows(i, core), :] = mid[...] + far[0]
+        pass_copy(i).wait_recv()
+        out[half_rows(i, 1 - core), :] = other[...] + far[1]
 
     for c in range(chunks):
-        forward(c)
+        forward_samples(c)
+    values = [forward_rays(c) for c in range(chunks)]
     pl.semaphore_wait(barrier, n_slab - 1 + len(mates))
-    for step in range(1, n_slab):
+    for step in range(n_slab - 1):
         exchange(step, me).start()
     gather_s[me] = send_s[...]
     for c in range(chunks):
+        slopes(c, values[c])
+    for c in range(chunks):
         hold(c)
-    for step in range(1, n_slab):
-        exchange(step, (me + n_slab - step) % n_slab).wait_recv()
+    for step in range(n_slab - 1):
+        exchange(step, origin(step)).wait_recv()
     cots = [compose(c) for c in range(chunks)]
-    for c in range(chunks):
-        coefficients(c, cots[c])
+    coefficients(0, cots[0])
+    backward_two(0)
+    coefficients(1, cots[1])
     grad_out(cots)
-    pair_copy(2).start()
-    backward_two(0)
-    swap_first(2)
-    for c in range(1, chunks):
-        backward_two(c)
+    send_own(2)
+    backward_two(1)
     pair_copy(1).start()
     backward_one(0)
-    swap_first(1)
-    for c in range(1, chunks):
-        backward_one(c)
+    lean_first()
+    backward_one(1)
     g1_s[...] = g1t_s[...].T
-    pair_copy(0).start()
-    swap_second(2)
-    swap_first(0)
-    swap_second(1)
-    finish_half(2)
-    swap_second(0)
-    finish_half(1)
-    finish_half(0)
+    send_own(0)
+    send_sums(2)
+    lean_second()
+    send_sums(0)
+    finish(2)
+    lean_third()
+    finish(0)
+    pass_copy(1).wait_recv()
     for i in (2, 1, 0):
-        pass_copy(i, 1 - core).wait_recv()
-    for i in (2, 1, 0):
-        pass_copy(i, core).wait_send()
+        pass_copy(i).wait_send()
         pair_copy(i).wait_send()
         for stage in range(2):
             for part in range(2):
-                swap_copy(i, stage, part).wait_send()
-    for step in range(1, n_slab):
+                for turn in range(1 if i == 1 else 2):
+                    swap_copy(i, stage, part, turn).wait_send()
+    for step in range(n_slab - 1):
         exchange(step, me).wait_send()
 
 
@@ -557,16 +613,17 @@
             pltpu.VMEM((out, hid), f32),
             *(pltpu.VMEM((r // 2, n), f32) for r, n in sizes),
             *(pltpu.VMEM((r // 2, n), f32) for r, n in sizes),
-            *(pltpu.VMEM((r // 2, n), f32) for r, n in sizes),
-            *(pltpu.VMEM((r // 2, n), f32) for r, n in sizes),
-            *(pltpu.VMEM((r // 2, n), f32) for r, n in sizes),
+            *(pltpu.VMEM((2, r // 2, n), f32) for r, n in sizes),
+            *(pltpu.VMEM((2, r // 2, n), f32) for r, n in sizes),
+            *(pltpu.VMEM((r // 2, n), f32) for r, n in sizes[::2]),
+            pltpu.VMEM((hid // 2, hid), f32),
             pltpu.SemaphoreType.DMA((chunks + 10,)),
             pltpu.SemaphoreType.DMA((n_slab,)),
             pltpu.SemaphoreType.DMA((n_slab,)),
             pltpu.SemaphoreType.DMA((3,)),
             pltpu.SemaphoreType.DMA((3,)),
-            pltpu.SemaphoreType.DMA((3, 2, 2)),
-            pltpu.SemaphoreType.DMA((3, 2, 2)),
+            pltpu.SemaphoreType.DMA((3, 2, 2, 2)),
+            pltpu.SemaphoreType.DMA((3, 2, 2, 2)),
             pltpu.SemaphoreType.DMA((3,)),
             pltpu.SemaphoreType.DMA((3,)),
         ]

time: 33.3 us -> 32.5 us (0.976)
  Pallas kernels: 32.5 us -> 31.8 us
    pallas_call x1, Pallas kernels: 31.7 us -> 31 us  [body(): pl.pallas_call(functools.partial(kernel, chunks, n_slab, n_tile), out_sha...]
where the time goes in v5:
time: 32.5 us; the launch traced here: 32.4 us
  Pallas kernels  31.8 us (98%)
  between operations  0.64 us (2%)
    pallas_call x1, Pallas kernels, body(): pl.pallas_call(functools.partial(kernel, chunks, n_slab, n_tile), out_sha...  31 us
    pallas_call x1, Pallas kernels, body(): pl.pallas_call(hand_on, out_shape=shapes, in_specs=[vmem] * 4, out_specs=...  0.79 us

profile of v5, /device:TPU:1, one launch (start us, length us, event | category | flops | bytes accessed | tf_op | source)
XLA Modules:
  0.0 32.4 jit_solution(2916292849241857109)
XLA Ops:
  0.6 31.0 %shard_map.138 = (f32[1,512]{1,0:T(1,128)S(1)}, f32[128,256]{1,0:T(8,128)S(1)}, f32[256,256]{1,0:T(8,128)S(1)}, f32[64,256]{1,0:T(8,128)S(1)}) custom-call(bf16[1,16,512,128]{3,2,1,0:T(8,128)(2,1)} %x_hbm.1, f32[1,16,512]{2,1,0:T(8,128)} %space_hbm.1, s32[1,512]{1,0:T(1,128)} %counts_hbm.1, s32[1,512]{1,0:T(1,128)} %bitcast.13, s32[1,512]{1,0:T(1,128)} %bitcast.14, ...), custom_call_target="tpu_custom_call" | custom-call | tf_op jit(solution)/shard_map/pallas_call | solution.py:636
  31.6 0.8 %shard_map.139 = (f32[1,512]{1,0:T(1,128)}, f32[128,256]{1,0:T(8,128)}, f32[256,256]{1,0:T(8,128)}, f32[64,256]{1,0:T(8,128)}) custom-call(f32[1,512]{1,0:T(1,128)S(1)} %get-tuple-element.12.refs_0_, f32[128,256]{1,0:T(8,128)S(1)} %get-tuple-element.13.refs_1_, f32[256,256]{1,0:T(8,128)S(1)} %get-tuple-element.14.refs_2_, ...), custom_call_target="tpu_custom_call" | custom-call | tf_op jit(solution)/shard_map/pallas_call | solution.py:658

commit v6 on v5

--- a/solution.py
+++ b/solution.py
@@ -111,16 +111,6 @@
     core, ypos = tile % 2, tile // 2
     n_y = n_tile // 2
 
-    barrier = pltpu.get_barrier_semaphore()
-    for step in range(1, n_slab):
-        pl.semaphore_signal(
-            barrier, inc=1, device_id={"slab": (me + step) % n_slab}, device_id_type=MESH
-        )
-    across = (ypos + 1 - 2 * (ypos % 2), n_y - 1 - ypos)
-    mates = [ypos * 2 + 1 - core] + [y * 2 + c for y in across for c in (core, 1 - core)]
-    for mate in mates:
-        pl.semaphore_signal(barrier, inc=1, device_id={"tile": mate}, device_id_type=MESH)
-
     small = [
         (w1_hbm.at[0], w1_s),
         (w2_hbm.at[0], w2_s),
@@ -148,6 +138,16 @@
         load.start()
     for load in x_loads[1:]:
         load.start()
+
+    barrier = pltpu.get_barrier_semaphore()
+    for step in range(1, n_slab):
+        pl.semaphore_signal(
+            barrier, inc=1, device_id={"slab": (me + step) % n_slab}, device_id_type=MESH
+        )
+    across = (ypos + 1 - 2 * (ypos % 2), n_y - 1 - ypos)
+    mates = [ypos * 2 + 1 - core] + [y * 2 + c for y in across for c in (core, 1 - core)]
+    for mate in mates:
+        pl.semaphore_signal(barrier, inc=1, device_id={"tile": mate}, device_id_type=MESH)
 
     loads[0].wait()
     w1t_s[...] = w1_s[...].T
@@ -299,21 +299,24 @@
             jnp.broadcast_to(ints_s[3, :, pl.ds(c * rays + (groups - 1) * LANES, LANES)], (8, LANES)),
         ) > 0
 
-        def step_of(run, item, item_first):
-            run_t, item_t = spread(run), spread(item)
+        def step_of(pair, item, item_first):
+            run, run_t = pair
+            item_t = spread(item)
             run_first = jnp.where(is_trans, 0.0, run) + run_t * item
             late_first = jnp.where(is_trans, 0.0, item) + item_t * run
-            return jnp.where(item_first, late_first, run_first)
-
-        low = high = identity
+            return jnp.where(item_first, late_first, run_first), run_t * item_t
+
+        low = high = (identity, jnp.ones_like(identity))
         for s in range(n_slab):
             t = n_slab - 1 - s
             low = step_of(low, jnp.where(s < me, gather_s[s, c], identity), rev)
             high = step_of(high, jnp.where(t > me, gather_s[t, c], identity), jnp.logical_not(rev))
+        low, low_t = low
+        high, high_t = high
         own = send_s[c]
         front = jnp.where(rev, high, low)
         back = jnp.where(rev, low, high)
-        front_t, own_t = spread(front), spread(own)
+        front_t, own_t = jnp.where(rev, high_t, low_t), spread(own)
         logits = front + front_t * own + (front_t * own_t) * back
         shade = 1.0 / (1.0 + jnp.exp(-logits))
         target = jnp.zeros((8, LANES), jnp.float32)

time: 32.5 us -> 32.3 us (level)
  no operation moved by 1% of the time
where the time goes in v6:
time: 32.3 us; the launch traced here: 32.2 us
  Pallas kernels  31.5 us (98%)
  between operations  0.64 us (2%)
    pallas_call x1, Pallas kernels, body(): pl.pallas_call(functools.partial(kernel, chunks, n_slab, n_tile), out_sha...  30.7 us
    pallas_call x1, Pallas kernels, body(): pl.pallas_call(hand_on, out_shape=shapes, in_specs=[vmem] * 4, out_specs=...  0.79 us

profile of v6, /device:TPU:1, one launch (start us, length us, event | category | flops | bytes accessed | tf_op | source)
XLA Modules:
  0.0 32.2 jit_solution(4366772935477237145)
XLA Ops:
  0.6 30.7 %shard_map.138 = (f32[1,512]{1,0:T(1,128)S(1)}, f32[128,256]{1,0:T(8,128)S(1)}, f32[256,256]{1,0:T(8,128)S(1)}, f32[64,256]{1,0:T(8,128)S(1)}) custom-call(bf16[1,16,512,128]{3,2,1,0:T(8,128)(2,1)} %x_hbm.1, f32[1,16,512]{2,1,0:T(8,128)} %space_hbm.1, s32[1,512]{1,0:T(1,128)} %counts_hbm.1, s32[1,512]{1,0:T(1,128)} %bitcast.13, s32[1,512]{1,0:T(1,128)} %bitcast.14, ...), custom_call_target="tpu_custom_call" | custom-call | tf_op jit(solution)/shard_map/pallas_call | solution.py:639
  31.4 0.8 %shard_map.139 = (f32[1,512]{1,0:T(1,128)}, f32[128,256]{1,0:T(8,128)}, f32[256,256]{1,0:T(8,128)}, f32[64,256]{1,0:T(8,128)}) custom-call(f32[1,512]{1,0:T(1,128)S(1)} %get-tuple-element.12.refs_0_, f32[128,256]{1,0:T(8,128)S(1)} %get-tuple-element.13.refs_1_, f32[256,256]{1,0:T(8,128)S(1)} %get-tuple-element.14.refs_2_, ...), custom_call_target="tpu_custom_call" | custom-call | tf_op jit(solution)/shard_map/pallas_call | solution.py:661

commit v7 on v6

--- a/solution.py
+++ b/solution.py
@@ -74,7 +74,6 @@
     send_s,
     gather_s,
     g1_s,
-    g1t_s,
     g2_s,
     g3_s,
     pair1_s,
@@ -398,8 +397,8 @@
         base = c * cols
         b1 = mm(w2_s[...], b2_s[:, pl.ds(base, cols)], NN).astype(jnp.bfloat16)
         b1 = jnp.where(h1_s[:, pl.ds(base, cols)] > 0, b1, 0)
-        part = mm(b1, x_s[c].reshape(cols, x_s.shape[3]), NN)
-        g1t_s[...] = part if c == 0 else g1t_s[...] + part
+        part = mm(x_s[c].reshape(cols, x_s.shape[3]), b1, ((0,), (1,)))
+        g1_s[...] = part if c == 0 else g1_s[...] + part
 
     grads = (
         (g1_s, pair1_s, near1_s, mid1_s, far1_s, other1_s, g1_out),
@@ -522,9 +521,9 @@
     for step in range(n_slab - 1):
         exchange(step, origin(step)).wait_recv()
     cots = [compose(c) for c in range(chunks)]
-    coefficients(0, cots[0])
+    for c in range(chunks):
+        coefficients(c, cots[c])
     backward_two(0)
-    coefficients(1, cots[1])
     grad_out(cots)
     send_own(2)
     backward_two(1)
@@ -532,7 +531,6 @@
     backward_one(0)
     lean_first()
     backward_one(1)
-    g1_s[...] = g1t_s[...].T
     send_own(0)
     send_sums(2)
     lean_second()
@@ -611,7 +609,6 @@
             pltpu.VMEM((chunks, 8, LANES), f32),
             pltpu.VMEM((n_slab, chunks, 8, LANES), f32),
             pltpu.VMEM((enc, hid), f32),
-            pltpu.VMEM((hid, enc), f32),
             pltpu.VMEM((hid, hid), f32),
             pltpu.VMEM((out, hid), f32),
             *(pltpu.VMEM((r // 2, n), f32) for r, n in sizes),

time: 32.3 us -> 32.3 us (level)
  no operation moved by 1% of the time
where the time goes in v7:
time: 32.3 us; the launch traced here: 32.2 us
  Pallas kernels  31.5 us (98%)
  between operations  0.64 us (2%)
    pallas_call x1, Pallas kernels, body(): pl.pallas_call(functools.partial(kernel, chunks, n_slab, n_tile), out_sha...  30.7 us
    pallas_call x1, Pallas kernels, body(): pl.pallas_call(hand_on, out_shape=shapes, in_specs=[vmem] * 4, out_specs=...  0.79 us

profile of v7, /device:TPU:1, one launch (start us, length us, event | category | flops | bytes accessed | tf_op | source)
XLA Modules:
  0.0 32.2 jit_solution(18412556794387403134)
XLA Ops:
  0.6 30.7 %shard_map.138 = (f32[1,512]{1,0:T(1,128)S(1)}, f32[128,256]{1,0:T(8,128)S(1)}, f32[256,256]{1,0:T(8,128)S(1)}, f32[64,256]{1,0:T(8,128)S(1)}) custom-call(bf16[1,16,512,128]{3,2,1,0:T(8,128)(2,1)} %x_hbm.1, f32[1,16,512]{2,1,0:T(8,128)} %space_hbm.1, s32[1,512]{1,0:T(1,128)} %counts_hbm.1, s32[1,512]{1,0:T(1,128)} %bitcast.13, s32[1,512]{1,0:T(1,128)} %bitcast.14, ...), custom_call_target="tpu_custom_call" | custom-call | tf_op jit(solution)/shard_map/pallas_call | solution.py:636
  31.4 0.8 %shard_map.139 = (f32[1,512]{1,0:T(1,128)}, f32[128,256]{1,0:T(8,128)}, f32[256,256]{1,0:T(8,128)}, f32[64,256]{1,0:T(8,128)}) custom-call(f32[1,512]{1,0:T(1,128)S(1)} %get-tuple-element.12.refs_0_, f32[128,256]{1,0:T(8,128)S(1)} %get-tuple-element.13.refs_1_, f32[256,256]{1,0:T(8,128)S(1)} %get-tuple-element.14.refs_2_, ...), custom_call_target="tpu_custom_call" | custom-call | tf_op jit(solution)/shard_map/pallas_call | solution.py:658
